TPU v7x, 512 devices: a whole 4x8x8 slice. The times are simulated.
512 devices in a mesh: row: 16 (over y, core), col: 32 (over z, x).
Axes of the slice: x: 4, y: 8, z: 8, core: 2. Of those that a mesh axis runs over, the one named last changes fastest.
Arguments:
- points: bfloat16 [128, 65536], P(None, ('row', 'col')), may hold values from -6 to 6
- inv_scale: float32 [128], replicated, may hold values from 0.07 to 0.22
- basis: bfloat16 [65536, 4096], P(('row', 'col')), may hold values from -0.25 to 0.25
- shrink: float32 [4096], replicated, may hold values from 0.02 to 1
- solution: float32 [33, 65536], P(None, ('row', 'col')), may hold values from -6 to 6
- residual: float32 [33, 65536], P(None, ('row', 'col')), may hold values from -6 to 6
- direction_prev: float32 [33, 65536], P(None, ('row', 'col')), may hold values from -6 to 6
- rz_prev: float32 [33], replicated, may hold values from 65536 to 262144
Outputs:
- solution_next: float32 [33, 65536], P(None, ('row', 'col'))
- residual_next: float32 [33, 65536], P(None, ('row', 'col'))
- direction: float32 [33, 65536], P(None, ('row', 'col'))
All inputs are finite; a program needn't handle non-finite values.
Results may differ from a plain program's by a relative error of at most 0.019.
Values may be sent and summed in bfloat16 or wider, within the bound.
A program may use at most 64 MiB of HBM per device.

v0:
```python
import jax
import jax.numpy as jnp
from jax import lax
from jax.sharding import PartitionSpec as P

noise_level = 0.25


def local(points, inv_scale, basis, shrink, solution, residual, direction_prev, rz_prev):
    scaled = (points * inv_scale[:, None]).astype(jnp.bfloat16)
    residual_bf = residual.astype(jnp.bfloat16)
    local_proj = jnp.dot(residual_bf, basis, preferred_element_type=jnp.float32)
    damping = shrink - 1.0
    projected = lax.psum(local_proj, ("row", "col"))
    correction = (damping[None, :] * projected).astype(jnp.bfloat16)
    precond = residual + jnp.dot(correction, basis.T, preferred_element_type=jnp.float32)
    precond_inner = lax.psum(jnp.sum(residual * precond, axis=1), ("row", "col"))
    direction = precond + (precond_inner / rz_prev)[:, None] * direction_prev
    direction_bf = direction.astype(jnp.bfloat16)
    row_points = lax.all_gather(scaled, "col", axis=1, tiled=True)
    row_sq = jnp.sum(jnp.square(row_points.astype(jnp.float32)), axis=0)
    rows_total = row_points.shape[1]
    width = min(1024, rows_total)
    direction_piece = lax.all_gather(direction_bf, "row", axis=1, tiled=True)
    column_pts = lax.all_gather(scaled, "row", axis=1, tiled=True)
    column_sq = jnp.sum(jnp.square(column_pts.astype(jnp.float32)), axis=0)
    results = []
    for offset in range(0, rows_total, width):
        rows = row_points[:, offset : offset + width]
        cross = lax.dot_general(
            column_pts, rows, (((0,), (0,)), ((), ())), preferred_element_type=jnp.float32
        )
        distance = jnp.maximum(
            column_sq[:, None] + row_sq[None, offset : offset + width] - 2.0 * cross, 0.0
        )
        tile = jnp.exp(-0.5 * distance).astype(jnp.bfloat16)
        results.append(jnp.dot(direction_piece, tile, preferred_element_type=jnp.float32))
    image_part = jnp.concatenate(results, axis=1)
    image = (
        lax.psum_scatter(
            image_part.astype(jnp.bfloat16), "col", scatter_dimension=1, tiled=True
        ).astype(jnp.float32)
        + noise_level * direction
    )
    curvature = lax.psum(jnp.sum(direction * image, axis=1), ("row", "col"))
    alpha = precond_inner / curvature
    solution_next = solution + alpha[:, None] * direction
    residual_next = residual - alpha[:, None] * image
    return (solution_next, residual_next, direction)


def solution(mesh):
    placed = (
        P(None, ("row", "col")),
        P(),
        P(("row", "col"), None),
        P(),
        P(None, ("row", "col")),
        P(None, ("row", "col")),
        P(None, ("row", "col")),
        P(),
    )
    return jax.shard_map(
        local,
        mesh=mesh,
        in_specs=placed,
        out_specs=(P(None, ("row", "col")), P(None, ("row", "col")), P(None, ("row", "col"))),
        check_vma=False,
    )
```

profile of v0, /device:TPU:1, one launch (start us, length us, event | category | flops | bytes accessed | tf_op | source)
XLA Modules:
  0.0 740.1 jit_solution(11344339179035116326)
XLA Ops:
  8.0 0.0 copy-start
  8.0 0.0 copy-start.4
  8.0 0.0 copy-start.8
  8.0 0.0 all-reduce.2.cloned.1.call-start
  8.1 1.2 copy-done
  9.2 1.9 fusion.17
  11.1 0.0 all-reduce.2.cloned.1.call-update
  11.1 0.0 all-gather.2.cloned.1.call-start
  11.2 0.0 copy-done.4
  11.2 0.7 multiply_convert_fusion.2
  11.9 0.0 all-gather.2.cloned.1.call-update
  11.9 0.0 reduce-scatter.4.cloned.1.call-start
  11.9 22.7 %all_gather.10 = bf16[128,2048]{1,0:T(8,128)(2,1)S(1)} all-gather(bf16[128,128]{1,0:T(8,128)(2,1)} %multiply_convert_fusion.2), channel_id=1, replica_groups=mesh['row'=16,'col'=32] {'row'}, dimensions={1}, use_global_device_ids=true | all-gather | bytes 557056 | tf_op jit(solution)/shard_map/all_gather | solution.py:25
  34.6 0.1 multiply_reduce_fusion.1
  34.8 256.8 %all-reduce.2.cloned.1.call-done = f32[33,4096]{1,0:T(8,128)} async-done(((f32[33,4096]{1,0:T(8,128)}), f32[33,4096]{1,0:T(8,128)}) %all-reduce.2.cloned.1.call-update) | async-done | bytes 540688 | tf_op jit(solution)/shard_map/psum | solution.py:14
  291.6 1.7 multiply_reduce_fusion.3
  293.3 97.0 %psum.22 = f32[33]{0:T(128)S(1)} all-reduce(f32[33]{0:T(128)S(1)} %get-tuple-element.11), channel_id=1, replica_groups=mesh['row'=16,'col'=32] {'row','col'}, use_global_device_ids=true, to_apply=%region_2.0 | all-reduce | flops 33 | bytes 264 | tf_op jit(solution)/shard_map/psum | solution.py:17
  390.3 0.1 fusion.31
  390.4 15.4 %all_gather.9 = bf16[33,2048]{1,0:T(8,128)(2,1)S(1)} all-gather(bf16[33,128]{1,0:T(8,128)(2,1)S(1)} %get-tuple-element.3), channel_id=1, replica_groups=mesh['row'=16,'col'=32] {'row'}, dimensions={1}, use_global_device_ids=true | all-gather | bytes 143616 | tf_op jit(solution)/shard_map/all_gather | solution.py:24
  405.7 1.5 multiply_reduce_fusion
  407.3 2.7 fusion.4
  410.0 2.7 fusion.5
  412.7 2.7 fusion.6
  415.5 2.7 fusion.7
  418.2 0.0 copy-start.5
  418.2 1.4 copy.11
  419.6 0.0 reduce-scatter.4.cloned.1.call-update
  419.7 210.6 %reduce-scatter.4.cloned.1.call-done = bf16[128,33]{1,0:T(8,128)(2,1)} async-done(((bf16[4096,33]{1,0:T(8,128)(2,1)}), bf16[128,33]{1,0:T(8,128)(2,1)}) %reduce-scatter.4.cloned.1.call-update) | async-done | bytes 8464
  630.3 0.8 copy.12
  631.1 0.1 multiply_reduce_fusion.2
  631.2 100.7 %psum.23 = f32[33]{0:T(128)S(1)} all-reduce(f32[33]{0:T(128)S(1)} %multiply_reduce_fusion.2), channel_id=1, replica_groups=mesh['row'=16,'col'=32] {'row','col'}, use_global_device_ids=true, to_apply=%region_7.0 | all-reduce | flops 33 | bytes 264 | tf_op jit(solution)/shard_map/psum | solution.py:45
  731.9 0.7 multiply_subtract_fusion
  (20 shorter events, 0.1 us)
Async XLA Ops:
  8.0 1.2 copy-start
  8.0 3.2 copy-start.4
  8.0 3.2 copy-start.8
  8.0 283.6 %all-reduce.2.cloned.1.call-start = ((), (), s32[]{:S(2)}) async-start(), calls=%async_computation.1 | async-start | bytes 1310720 | tf_op jit(solution)/shard_map/psum | solution.py:14
  11.1 23.7 %copy-start.7 = (f32[4096]{0:T(1024)S(1)}, f32[4096]{0:T(1024)}, u32[]{:S(2)}) copy-start(f32[4096]{0:T(1024)} %param.11) | copy-start | bytes 49156
  11.1 280.5 %copy-start.3 = (f32[33,128]{1,0:T(8,128)S(1)}, f32[33,128]{1,0:T(8,128)}, u32[]{:S(2)}) copy-start(f32[33,128]{1,0:T(8,128)} %param.13) | copy-start | bytes 50692
  11.1 394.6 %all-gather.2.cloned.1.call-start = ((), (), s32[]{:S(2)}) async-start(), calls=%async_computation.2 | async-start | bytes 1081344 | tf_op jit(solution)/shard_map/all_gather | solution.py:20
  11.9 618.4 %reduce-scatter.4.cloned.1.call-start = ((), (), s32[]{:S(2)}) async-start(), calls=%async_computation.3 | async-start | bytes 1081344
  34.6 355.6 %copy-start.9 = (f32[33]{0:T(128)S(1)}, f32[33]{0:T(128)}, u32[]{:S(2)}) copy-start(f32[33]{0:T(128)} %param.15) | copy-start | bytes 400
  34.6 355.6 %copy-start.6 = (f32[33,128]{1,0:T(8,128)S(1)}, f32[33,128]{1,0:T(8,128)}, u32[]{:S(2)}) copy-start(f32[33,128]{1,0:T(8,128)} %param.14) | copy-start | bytes 50692
  390.4 341.6 %copy-start.2 = (f32[33,128]{1,0:T(8,128)}, f32[33,128]{1,0:T(8,128)S(1)}, u32[]{:S(2)}) copy-start(f32[33,128]{1,0:T(8,128)S(1)} %get-tuple-element.4) | copy-start | bytes 50692
  405.7 1.6 copy-start.1
  418.2 313.7 %copy-start.5 = (f32[33,128]{1,0:T(8,128)S(1)}, f32[33,128]{1,0:T(8,128)}, u32[]{:S(2)}) copy-start(f32[33,128]{1,0:T(8,128)} %param.12) | copy-start | bytes 50692
Sparse Core Ops, SparseCore 0:
  13.8 277.7 all-reduce.1
Sparse Core Ops, SparseCore 1:
  15.1 78.6 all-gather.1
  419.7 210.5 reduce-scatter.3
where the time goes:
time: 740 us
  waiting for transfers between devices  467 us (63%)
  blocking collectives  236 us (32%)
  between operations  15.6 us (2%)
  matrix products  14.4 us (2%)
    psum x1, waiting for transfers between devices, local(): projected = lax.psum(local_proj, ('row', 'col'))  257 us
    unnamed x4, waiting for transfers between devices  211 us
    psum x1, blocking collectives, local(): curvature = lax.psum(jnp.sum(direction * image, axis=1), ('row', 'col'))  101 us
    psum x1, blocking collectives, local(): lax.psum(jnp.sum(residual * precond, axis=1), ('row', 'col'))  97 us
    all_gather x1, blocking collectives, local(): column_pts = lax.all_gather(scaled, 'row', axis=1, tiled=True)  22.7 us
    all_gather x1, blocking collectives, local(): direction_piece = lax.all_gather(direction_bf, 'row', axis=1, tiled=True)  15.4 us
  transfers between devices with their start and end apart: 3, of which 2 were waited for; matrix products, arithmetic and copies ran while one was open for 0% of the time, Pallas kernels for 0%

commit v1 on v0

v1 whole, which is shorter than its diff:
```python
import functools

import jax
import jax.numpy as jnp
from jax import lax
from jax.experimental import pallas as pl
from jax.experimental.pallas import tpu as pltpu
from jax.sharding import PartitionSpec as P

MESH = pl.DeviceIdType.MESH
BF = jnp.bfloat16
F32 = jnp.float32
NOISE = 0.25
G = 16
L = 128
HALF = G * L
ROWS = 48
RHS = 33
NORM_ROW = 40
IP_ROW = 44


def split3(v):
    hi = v.astype(BF).astype(F32)
    mid = (v - hi).astype(BF).astype(F32)
    return hi, mid, v - hi - mid


def kernel(
    points, inv_scale, basis_hbm, shrink, sol, res, prev, rz,
    sol_out, res_out, dir_out,
    basis, r48, s_own, st_own, si, sj, sqj, tile,
    p_send, p_recv, p_half, e1, e2_send, e2, corr_own, corr, d48, d_own, dj,
    im_send, im_recv, im_own, e5_send, e5, c1_send, c1, c2_send, c2,
    basis_sem, ssem, rsem,
):
    row = lax.axis_index("row")
    col = lax.axis_index("col")
    core = row % 2
    y = row // 2
    z = col // 4
    x = col % 4
    xa = x // 2
    xb = ((x + 1) // 2) % 2
    g1 = z * 2 + xb
    g2 = y * 2 + xa

    def dev1(g):
        b = g % 2
        return (row, (g // 2) * 4 + 3 * xa + b - 2 * xa * b)

    def dev2(g, c):
        a = g % 2
        return ((g // 2) * 2 + c, z * 4 + 3 * a + xb - 2 * a * xb)

    other = 1 - core
    twin = (y * 2 + other, col)

    bar = pltpu.get_barrier_semaphore()
    cp = pltpu.make_async_copy(basis_hbm, basis, basis_sem)
    cp.start()
    pl.semaphore_signal(bar, inc=1, device_id=twin, device_id_type=MESH)

    def sig(s, _):
        pl.semaphore_signal(bar, inc=1, device_id=dev1((g1 + s) % G), device_id_type=MESH)
        pl.semaphore_signal(bar, inc=1, device_id=dev2((g2 + s) % G, core), device_id_type=MESH)
        pl.semaphore_signal(bar, inc=1, device_id=dev2((g2 + s) % G, other), device_id_type=MESH)
        return 0

    lax.fori_loop(1, G, sig, 0)

    def lanes(g):
        return pl.ds(pl.multiple_of(g * L, L), L)

    def send(i, src, dst, dev):
        pltpu.make_async_remote_copy(
            src_ref=src, dst_ref=dst, send_sem=ssem.at[i], recv_sem=rsem.at[i],
            device_id=dev, device_id_type=MESH,
        ).start()

    def recv_wait(i, ref):
        pltpu.make_async_copy(ref, ref, rsem.at[i]).wait()

    def send_wait(i, ref):
        pltpu.make_async_copy(ref, ref, ssem.at[i]).wait()

    inv_col = jnp.broadcast_to(inv_scale[...], (L, L)).T
    scaled = (points[...].astype(F32) * inv_col).astype(BF)
    s_own[...] = scaled
    st_own[...] = scaled.astype(F32).T.astype(BF)
    si[0, :, lanes(g1)] = s_own[...]
    sj[lanes(g2), :] = st_own[...]

    r48[...] = jnp.zeros((ROWS, L), F32)
    r48[0:RHS, :] = res[...]
    r = r48[...]
    r_bf = r.astype(BF)
    rid = lax.broadcasted_iota(jnp.int32, (ROWS, L), 0)
    lid = lax.broadcasted_iota(jnp.int32, (ROWS, L), 1)
    eye = rid == lid

    def to_row(c):
        return jnp.sum(jnp.where(eye, c, 0.0), axis=0, keepdims=True)

    def to_col(v):
        return jnp.sum(jnp.where(eye, v, 0.0), axis=1, keepdims=True)

    norm_row = to_row(jnp.sum(r * r, axis=1, keepdims=True))
    norm_in = jnp.where(rid == NORM_ROW, norm_row, 0.0)

    W = 256
    cp.wait()

    def proj_twin(n, _):
        o = pl.multiple_of(other * HALF + n * W, W)
        p_send[:, pl.ds(pl.multiple_of(n * W, W), W)] = jnp.dot(
            r_bf, basis[:, pl.ds(o, W)], preferred_element_type=F32
        )
        return 0

    lax.fori_loop(0, HALF // W, proj_twin, 0)
    for g in range(G):
        blk = p_send[:, g * L : (g + 1) * L]
        p_send[:, g * L : (g + 1) * L] = blk + norm_in

    pl.semaphore_wait(bar, 3 * (G - 1) + 1)
    send(0, p_send, p_recv, twin)

    def proj_own(n, _):
        o = pl.multiple_of(core * HALF + n * W, W)
        d = pl.ds(pl.multiple_of(n * W, W), W)
        im_own[:, d] = jnp.dot(r_bf, basis[:, pl.ds(o, W)], preferred_element_type=F32)
        return 0

    lax.fori_loop(0, HALF // W, proj_own, 0)
    recv_wait(0, p_recv)
    for g in range(G):
        d = slice(g * L, (g + 1) * L)
        v = im_own[:, d] + p_recv[:, d] + norm_in
        nrow = v[NORM_ROW : NORM_ROW + 1, :]
        hi, mid, lo = split3(nrow)
        v = jnp.where(rid == NORM_ROW, hi, v)
        v = jnp.where(rid == NORM_ROW + 1, mid, v)
        v = jnp.where(rid == NORM_ROW + 2, lo, v)
        p_half[:, d] = v.astype(BF)

    def send1(s, _):
        g = (g1 + s) % G
        send(1, p_half.at[:, lanes(g)], e1.at[g1], dev1(g))
        return 0

    lax.fori_loop(1, G, send1, 0)

    def send_pts(s, _):
        ga = (g1 + s) % G
        gb = (g2 + s) % G
        send(2, s_own, si.at[0, :, lanes(g1)], dev1(ga))
        send(3, st_own, sj.at[lanes(g2), :], dev2(gb, core))
        return 0

    lax.fori_loop(1, G, send_pts, 0)

    e1[g1] = p_half[:, lanes(g1)]
    recv_wait(1, e1.at[pl.ds(0, G - 1)])

    def resplit(v):
        n = jnp.sum(jnp.where((rid >= NORM_ROW) & (rid < NORM_ROW + 3), v, 0.0), axis=0, keepdims=True)
        return n

    acc = e1[0].astype(F32)
    for g in range(1, G):
        acc = acc + e1[g].astype(F32)
    hi, mid, lo = split3(resplit(acc))
    acc = jnp.where(rid == NORM_ROW, hi, acc)
    acc = jnp.where(rid == NORM_ROW + 1, mid, acc)
    acc = jnp.where(rid == NORM_ROW + 2, lo, acc)
    e2_send[...] = acc.astype(BF)

    def send2(s, _):
        send(4, e2_send, e2.at[g2], dev2((g2 + s) % G, core))
        return 0

    lax.fori_loop(1, G, send2, 0)
    e2[g2] = e2_send[...]
    recv_wait(4, e2.at[pl.ds(0, G - 1)])
    acc = e2[0].astype(F32)
    for g in range(1, G):
        acc = acc + e2[g].astype(F32)
    norm_tot = resplit(acc)
    damping = shrink[pl.ds(core * G + g1, 1), :] - 1.0
    proj = jnp.where(rid < RHS, acc, 0.0)
    cor = (damping * proj).astype(BF)
    ip = to_row(jnp.sum(cor.astype(F32) * proj, axis=1, keepdims=True))
    hi, mid, lo = split3(ip)
    cf = cor.astype(F32)
    cf = jnp.where(rid == IP_ROW, hi, cf)
    cf = jnp.where(rid == IP_ROW + 1, mid, cf)
    cf = jnp.where(rid == IP_ROW + 2, lo, cf)
    corr_own[...] = cf.astype(BF)

    def send3(s, _):
        send(5, corr_own, corr.at[:, lanes(core * G + g1)], dev1((g1 + s) % G))
        return 0

    lax.fori_loop(1, G, send3, 0)
    corr[:, lanes(core * G + g1)] = corr_own[...]

    recv_wait(2, si.at[0, :, pl.ds(0, HALF - L)])
    recv_wait(3, sj.at[pl.ds(0, HALF - L), :])
    send(6, si.at[0], si.at[1], twin)

    recv_wait(5, corr.at[:, pl.ds(0, HALF - L)])
    half = corr.at[:, pl.ds(pl.multiple_of(core * HALF, HALF), HALF)]
    send(7, half, half, twin)

    def sq_rows(n, _):
        d = lanes(n)
        v = sj[d, :].astype(F32)
        sqj[d, :] = jnp.broadcast_to(0.5 * jnp.sum(v * v, axis=1, keepdims=True), (L, L))
        return 0

    lax.fori_loop(0, G, sq_rows, 0)

    def build(h):
        def outer(n, _):
            d = pl.ds(pl.multiple_of(n * W, W), W)
            pts = si[h, :, d]
            pf = pts.astype(F32)
            sq = 0.5 * jnp.sum(pf * pf, axis=0, keepdims=True)

            def inner(m, _):
                e = pl.ds(pl.multiple_of(m * W, W), W)
                cross = jnp.dot(sj[e, :], pts, preferred_element_type=F32)
                sc = sqj[e, :]
                sc = jnp.concatenate([sc, sc], axis=1)
                tile[h, e, d] = jnp.exp(jnp.minimum(cross - sc - sq, 0.0)).astype(BF)
                return 0

            lax.fori_loop(0, HALF // W, inner, 0)
            return 0

        lax.fori_loop(0, HALF // W, outer, 0)

    build(0)

    recv_wait(7, half)
    full = corr[...]
    ipr = jnp.zeros((1, L), F32)
    for g in range(2 * G):
        blk = corr[IP_ROW : IP_ROW + 3, g * L : (g + 1) * L].astype(F32)
        ipr = ipr + jnp.sum(blk, axis=0, keepdims=True)
    ip_col = to_col(ipr + norm_tot)
    cid = lax.broadcasted_iota(jnp.int32, (ROWS, 1), 0)
    rzp = jnp.concatenate([rz[...], jnp.ones((1, L - RHS), F32)], axis=1)
    rz_col = jnp.where(cid < RHS, to_col(rzp), 1.0)
    pre = r + lax.dot_general(full, basis[...], (((1,), (1,)), ((), ())), preferred_element_type=F32)
    d48[...] = jnp.zeros((ROWS, L), F32)
    d48[0:RHS, :] = prev[...]
    direction = pre + (ip_col / rz_col) * d48[...]
    direction = jnp.where(rid < RHS, direction, 0.0)
    d48[...] = direction
    d_own[...] = direction.astype(BF)

    def send4(s, _):
        send(8, d_own, dj.at[:, lanes(g2)], dev2((g2 + s) % G, core))
        return 0

    lax.fori_loop(1, G, send4, 0)
    dj[:, lanes(g2)] = d_own[...]

    recv_wait(6, si.at[1])
    build(1)
    recv_wait(8, dj.at[:, pl.ds(0, HALF - L)])

    def image(h, out):
        def step(n, _):
            d = pl.ds(pl.multiple_of(n * W, W), W)
            out[:, d] = jnp.dot(dj[...], tile[h, :, d], preferred_element_type=F32)
            return 0

        lax.fori_loop(0, HALF // W, step, 0)

    image(1, im_send)
    send(9, im_send, im_recv, twin)
    image(0, im_own)
    recv_wait(9, im_recv)
    e5_send[...] = (im_own[...] + im_recv[...]).astype(BF)

    def send5(s, _):
        g = (g1 + s) % G
        send(10, e5_send.at[:, lanes(g)], e5.at[g1], dev1(g))
        return 0

    lax.fori_loop(1, G, send5, 0)
    e5[g1] = e5_send[:, lanes(g1)]
    recv_wait(10, e5.at[pl.ds(0, G - 1)])
    acc = e5[0].astype(F32)
    for g in range(1, G):
        acc = acc + e5[g].astype(F32)
    direction = d48[...]
    img = acc + NOISE * direction

    cur = to_row(jnp.sum(direction * img, axis=1, keepdims=True))
    c1_send[...] = jnp.broadcast_to(cur, (8, L))

    def send6(s, _):
        send(11, c1_send, c1.at[g1], dev1((g1 + s) % G))
        return 0

    lax.fori_loop(1, G, send6, 0)
    c1[g1] = c1_send[...]
    recv_wait(11, c1.at[pl.ds(0, G - 1)])
    c2_send[...] = jnp.sum(c1[...], axis=0)

    def send7(s, _):
        g = (g2 + s) % G
        send(12, c2_send, c2.at[core * G + g2], dev2(g, core))
        send(12, c2_send, c2.at[core * G + g2], dev2(g, other))
        return 0

    send(12, c2_send, c2.at[core * G + g2], twin)
    lax.fori_loop(1, G, send7, 0)
    c2[core * G + g2] = c2_send[...]
    recv_wait(12, c2.at[pl.ds(0, 2 * G - 1)])
    cur = jnp.sum(c2[...], axis=0)[0:1, :]
    cur_col = jnp.where(cid < RHS, to_col(cur), 1.0)
    alpha = ip_col / cur_col
    dir_out[...] = direction[0:RHS, :]
    sol_out[...] = sol[...] + (alpha * direction)[0:RHS, :]
    res_out[...] = res[...] - (alpha * img)[0:RHS, :]

    send_wait(0, p_send)
    send_wait(1, e1.at[pl.ds(0, G - 1)])
    send_wait(2, si.at[0, :, pl.ds(0, HALF - L)])
    send_wait(3, sj.at[pl.ds(0, HALF - L), :])
    send_wait(4, e2.at[pl.ds(0, G - 1)])
    send_wait(5, corr.at[:, pl.ds(0, HALF - L)])
    send_wait(6, si.at[0])
    send_wait(7, half)
    send_wait(8, dj.at[:, pl.ds(0, HALF - L)])
    send_wait(9, im_send)
    send_wait(10, e5.at[pl.ds(0, G - 1)])
    send_wait(11, c1.at[pl.ds(0, G - 1)])
    send_wait(12, c2.at[pl.ds(0, 2 * G - 1)])


def solution(mesh):
    axes = ("row", "col")
    pts = P(None, axes)
    placed = (pts, P(), P(axes, None), P(), pts, pts, pts, P())

    def step(points, inv_scale, basis, shrink, sol, res, prev, rz):
        rank = basis.shape[1]
        out = jax.ShapeDtypeStruct((RHS, L), F32)
        v = pl.BlockSpec(memory_space=pltpu.VMEM)
        return pl.pallas_call(
            kernel,
            out_shape=(out, out, out),
            in_specs=[v, v, pl.BlockSpec(memory_space=pl.ANY), v, v, v, v, v],
            out_specs=(v, v, v),
            scratch_shapes=[
                pltpu.VMEM((L, rank), BF),
                pltpu.VMEM((ROWS, L), F32),
                pltpu.VMEM((L, L), BF),
                pltpu.VMEM((L, L), BF),
                pltpu.VMEM((2, L, HALF), BF),
                pltpu.VMEM((HALF, L), BF),
                pltpu.VMEM((HALF, L), F32),
                pltpu.VMEM((2, HALF, HALF), BF),
                pltpu.VMEM((ROWS, HALF), F32),
                pltpu.VMEM((ROWS, HALF), F32),
                pltpu.VMEM((ROWS, HALF), BF),
                pltpu.VMEM((G, ROWS, L), BF),
                pltpu.VMEM((ROWS, L), BF),
                pltpu.VMEM((G, ROWS, L), BF),
                pltpu.VMEM((ROWS, L), BF),
                pltpu.VMEM((ROWS, rank), BF),
                pltpu.VMEM((ROWS, L), F32),
                pltpu.VMEM((ROWS, L), BF),
                pltpu.VMEM((ROWS, HALF), BF),
                pltpu.VMEM((ROWS, HALF), F32),
                pltpu.VMEM((ROWS, HALF), F32),
                pltpu.VMEM((ROWS, HALF), F32),
                pltpu.VMEM((ROWS, HALF), BF),
                pltpu.VMEM((G, ROWS, L), BF),
                pltpu.VMEM((8, L), F32),
                pltpu.VMEM((G, 8, L), F32),
                pltpu.VMEM((8, L), F32),
                pltpu.VMEM((2 * G, 8, L), F32),
                pltpu.SemaphoreType.DMA,
                pltpu.SemaphoreType.DMA((13,)),
                pltpu.SemaphoreType.DMA((13,)),
            ],
            compiler_params=pltpu.CompilerParams(
                collective_id=0, has_side_effects=True, vmem_limit_bytes=48 * 1024 * 1024
            ),
            name="cg_step",
        )(
            points, inv_scale.reshape(1, L), basis, shrink.reshape(rank // L, L),
            sol, res, prev, rz.reshape(1, RHS),
        )

    return jax.shard_map(
        step, mesh=mesh, in_specs=placed, out_specs=(pts, pts, pts), check_vma=False
    )
```

time: 740 us -> 108 us (0.15)
  waiting for transfers between devices: 467 us -> 0 us
  blocking collectives: 236 us -> 0 us
  Pallas kernels: 0 us -> 99.3 us
  between operations: 15.6 us -> 0.67 us
  matrix products: 14.4 us -> 0 us
    psum x1 -> x0, waiting for transfers between devices: 257 us -> none  [local(): projected = lax.psum(local_proj, ('row', 'col'))]
    unnamed x4 -> x0, waiting for transfers between devices: 211 us -> none
    psum x2 -> x0, blocking collectives: 198 us -> none  [the longest x1 101 us: local(): curvature = lax.psum(jnp.sum(direction * image, axis=1), ('row', 'col'))]
    pallas_call x0 -> x1, Pallas kernels: none -> 99.3 us  [step(): pl.pallas_call(kernel, out_shape=(out, out, out), in_specs=[v, v, pl.Bloc...]
    all_gather x2 -> x0, blocking collectives: 38 us -> none  [the longest x1 22.7 us: local(): column_pts = lax.all_gather(scaled, 'row', axis=1, tiled=True)]
    dot_general x6 -> x0, matrix products: 14.4 us -> none  [the longest x4 10.9 us: local(): jnp.dot(direction_piece, tile, preferred_element_type=jnp.float32)]
  transfers between devices with their start and end apart: 3 -> 0, of which waited for: 2 -> 0; matrix products, arithmetic and copies ran while one was open for 0% -> 0% of each run, Pallas kernels for 0% -> 0%
where the time goes in v1:
time: 108 us; the launch traced here: 107 us
  Pallas kernels  99.3 us (92%)
  local copies, waits for them, and re-layouts  7.36 us (7%)
    pallas_call x1, Pallas kernels, step(): pl.pallas_call(kernel, out_shape=(out, out, out), in_specs=[v, v, pl.Bloc...  99.3 us
    unnamed x19, local copies, waits for them, and re-layouts  7.36 us

profile of v1, /device:TPU:1, one launch (start us, length us, event | category | flops | bytes accessed | tf_op | source)
XLA Modules:
  0.0 107.3 jit_solution(13740095355263111839)
XLA Ops:
  0.6 0.0 copy-start.6
  0.6 0.0 copy-start.7
  0.7 0.6 copy-done.6
  1.3 0.0 copy-done.7
  1.3 0.0 copy-start
  1.3 1.2 %copy-done = bf16[128,4096]{1,0:T(8,128)(2,1)S(1)} copy-done((bf16[128,4096]{1,0:T(8,128)(2,1)S(1)}, bf16[128,4096]{1,0:T(8,128)(2,1)}, u32[]{:S(2)}) %copy-start) | copy-done | bytes 1048600
  2.5 0.0 copy-start.1
  2.5 0.8 copy-done.1
  3.3 0.0 copy-start.2
  3.3 0.7 copy-done.2
  4.0 0.0 copy-start.3
  4.0 0.7 copy-done.3
  4.7 0.0 copy-start.4
  4.7 0.7 copy-done.4
  5.5 0.0 copy-start.5
  5.5 0.7 copy-done.5
  6.2 99.3 %cg_step.1 = (f32[33,128]{1,0:T(8,128)S(1)}, f32[33,128]{1,0:T(8,128)S(1)}, f32[33,128]{1,0:T(8,128)S(1)}) custom-call(bf16[128,128]{1,0:T(8,128)(2,1)S(1)} %copy-done.1, f32[1,128]{1,0:T(1,128)S(1)} %bitcast.4, bf16[128,4096]{1,0:T(8,128)(2,1)S(1)} %copy-done, f32[32,128]{1,0:T(8,128)S(1)} %bitcast.3, f32[33,128]{1,0:T(8,128)S(1)} %copy-done.2, ...), custom_call_target="tpu_custom_call" | custom-call | tf_op jit(solution)/shard_map/cg_step/pallas_call | solution.py:356
  105.5 0.6 copy.14
  106.1 0.6 copy.15
  106.7 0.6 copy.16
Async XLA Ops:
  0.6 0.7 copy-start.6
  0.6 0.7 copy-start.7
  1.3 1.2 %copy-start = (bf16[128,4096]{1,0:T(8,128)(2,1)S(1)}, bf16[128,4096]{1,0:T(8,128)(2,1)}, u32[]{:S(2)}) copy-start(bf16[128,4096]{1,0:T(8,128)(2,1)} %basis_hbm.1) | copy-start | bytes 3145732
  2.5 0.8 copy-start.1
  3.3 0.7 copy-start.2
  4.0 0.7 copy-start.3
  4.7 0.7 copy-start.4
  5.5 0.7 copy-start.5

commit v2 on v0

v2 whole, which is shorter than its diff:
```python
import jax
import jax.numpy as jnp
from jax import lax
from jax.experimental import pallas as pl
from jax.experimental.pallas import tpu as pltpu
from jax.sharding import PartitionSpec as P

MESH = pl.DeviceIdType.MESH
BF = jnp.bfloat16
F32 = jnp.float32
NOISE = 0.25
G = 16
L = 128
HALF = G * L
RHS = 33
ROWS = 40
NORM = 33
INNER = 36


def split3(v):
    hi = v.astype(BF).astype(F32)
    mid = (v - hi).astype(BF).astype(F32)
    return hi, mid, v - hi - mid


def kernel(
    points, inv_scale, basis_hbm, shrink, res, prev, rz,
    pre_out, beta_out, alpha_out, img_out,
    basis, r40, s_own, st_own, si, sj, tile,
    p_send, p_recv, p_half, e1, e2_send, e2, corr_own, corr, d40, d_own, dj, di,
    im_send, im_recv, im_own, e5_send, e5, c2_send, c2, c3_send, c3,
    basis_sem, ssem, rsem,
):
    row = lax.axis_index("row")
    col = lax.axis_index("col")
    core = row % 2
    y = row // 2
    z = col // 4
    x = col % 4
    xa = x // 2
    xb = ((x + 1) // 2) % 2
    g1 = z * 2 + xb
    g2 = y * 2 + xa
    other = 1 - core
    twin = (y * 2 + other, col)

    def far(t):
        return (4 + ((t + 1) // 2) * (1 - 2 * (t % 2))) % 8

    def dev1(t, flip):
        zz = (z + far(t)) % 8
        b = (xb + flip) % 2
        return (row, zz * 4 + 3 * xa + b - 2 * xa * b), zz * 2 + b

    def dev2(t, flip):
        yy = (y + far(t)) % 8
        a = (xa + flip) % 2
        return (yy * 2 + core, z * 4 + 3 * a + xb - 2 * a * xb), yy * 2 + a

    def each(dev, fn, lo=0, hi=8):
        def body(t, _):
            fn(*dev(t, 1))
            fn(*dev(t, 0))
            return 0

        lax.fori_loop(lo, min(hi, 7), body, 0)
        if hi == 8:
            fn(*dev(7, 1))

    def lanes(g):
        return pl.ds(pl.multiple_of(g * L, L), L)

    def send(i, src, dst, dev):
        pltpu.make_async_remote_copy(
            src_ref=src, dst_ref=dst, send_sem=ssem.at[i], recv_sem=rsem.at[i],
            device_id=dev, device_id_type=MESH,
        ).start()

    sent, coming = {}, {}

    def expect(i, ref):
        sent[i] = ref
        coming[i] = ref

    def recv_wait(i):
        ref = coming.pop(i)
        pltpu.make_async_copy(ref, ref, rsem.at[i]).wait()

    def drain():
        for i in list(coming):
            recv_wait(i)
        for i, ref in sent.items():
            pltpu.make_async_copy(ref, ref, ssem.at[i]).wait()

    bar = pltpu.get_barrier_semaphore()
    cp = pltpu.make_async_copy(basis_hbm, basis, basis_sem)
    cp.start()

    def signal(dev, _):
        pl.semaphore_signal(bar, inc=1, device_id=dev, device_id_type=MESH)

    signal(twin, 0)
    each(dev1, signal)
    each(dev2, signal)

    inv_col = jnp.broadcast_to(inv_scale[...], (L, L)).T
    scaled = (points[...].astype(F32) * inv_col).astype(BF)
    s_own[...] = scaled
    st_own[...] = scaled.astype(F32).T.astype(BF)
    si[0, 0:L, lanes(g1)] = s_own[...]
    sj[lanes(g2), 0:L] = st_own[...]
    for h in range(2):
        si[h, L : 2 * L, :] = jnp.zeros((L, HALF), BF)

    r40[...] = jnp.zeros((ROWS, L), F32)
    r40[0:RHS, :] = res[...]
    r = r40[...]
    r_bf = r.astype(BF)
    rid = lax.broadcasted_iota(jnp.int32, (ROWS, L), 0)
    lid = lax.broadcasted_iota(jnp.int32, (ROWS, L), 1)
    cid = lax.broadcasted_iota(jnp.int32, (ROWS, 1), 0)
    eye = rid == lid

    def to_row(c):
        return jnp.sum(jnp.where(eye, c, 0.0), axis=0, keepdims=True)

    def to_col(v):
        return jnp.sum(jnp.where(eye, v, 0.0), axis=1, keepdims=True)

    def put(v, base, line):
        hi, mid, lo = split3(line)
        v = jnp.where(rid == base, hi, v)
        v = jnp.where(rid == base + 1, mid, v)
        return jnp.where(rid == base + 2, lo, v)

    def take(v, base):
        return jnp.sum(jnp.where((rid >= base) & (rid < base + 3), v, 0.0), axis=0, keepdims=True)

    zero = jnp.zeros((ROWS, L), F32)
    norm = to_row(jnp.sum(r * r, axis=1, keepdims=True))
    norm_in = put(zero, NORM, norm)

    cp.wait()

    def half_of(c):
        return pl.ds(pl.multiple_of(c * HALF, HALF), HALF)

    proj_t = jnp.dot(r_bf, basis[:, half_of(other)], preferred_element_type=F32)
    for g in range(G):
        d = slice(g * L, (g + 1) * L)
        p_send[:, d] = (proj_t[:, d] + norm_in).astype(BF)
    im_own[...] = jnp.dot(r_bf, basis[:, half_of(core)], preferred_element_type=F32)

    pl.semaphore_wait(bar, 2 * (G - 1) + 1)
    send(0, p_send, p_recv, twin)
    expect(0, p_send)

    def send_j(dev, g):
        send(3, st_own, sj.at[lanes(g2), pl.ds(0, L)], dev)

    def send_i(dev, g):
        send(2, s_own, si.at[0, pl.ds(0, L), lanes(g1)], dev)

    each(dev2, send_j)
    expect(3, sj.at[pl.ds(0, HALF - L), pl.ds(0, L)])
    each(dev1, send_i, 5, 8)
    expect(2, si.at[0, pl.ds(0, L), pl.ds(0, HALF - L)])

    recv_wait(0)
    norm_in = put(zero, NORM, norm + take(p_recv[:, 0:L].astype(F32), NORM))
    for g in range(G):
        d = slice(g * L, (g + 1) * L)
        v = im_own[:, d] + p_recv[:, d].astype(F32)
        p_half[:, d] = jnp.where(rid < RHS, v, norm_in).astype(BF)

    def send1(dev, g):
        send(1, p_half.at[:, lanes(g)], e1.at[g1], dev)

    each(dev1, send1)
    expect(1, e1.at[pl.ds(0, G - 1)])
    e1[g1] = p_half[:, lanes(g1)]

    def total(ref):
        acc = ref[0].astype(F32)
        for g in range(1, G):
            acc = acc + ref[g].astype(F32)
        return acc

    recv_wait(1)
    acc = total(e1)
    e2_send[...] = put(acc, NORM, take(acc, NORM)).astype(BF)

    def send2(dev, g):
        send(4, e2_send, e2.at[g2], dev)

    each(dev2, send2)
    expect(4, e2.at[pl.ds(0, G - 1)])
    each(dev1, send_i, 0, 5)
    e2[g2] = e2_send[...]
    recv_wait(4)
    acc = total(e2)
    norm_all = take(acc, NORM)
    proj = jnp.where(rid < RHS, acc, 0.0)
    cor = ((shrink[pl.ds(core * G + g1, 1), :] - 1.0) * proj).astype(BF).astype(F32)
    inner = to_row(jnp.sum(cor * proj, axis=1, keepdims=True))
    corr_own[...] = put(cor, INNER, inner).astype(BF)

    def send3(dev, g):
        send(5, corr_own, corr.at[:, lanes(core * G + g1)], dev)

    each(dev1, send3)
    expect(5, corr.at[:, pl.ds(0, HALF - L)])
    corr[:, lanes(core * G + g1)] = corr_own[...]

    lane = lax.broadcasted_iota(jnp.int32, (L, L), 1)

    def aug_j():
        def body(n, _):
            v = sj[lanes(n), 0:L].astype(F32)
            hi, mid, lo = split3(jnp.broadcast_to(-0.5 * jnp.sum(v * v, axis=1, keepdims=True), (L, L)))
            ext = jnp.where(lane == 0, hi, jnp.where(lane == 1, mid, jnp.where(lane == 2, lo, 1.0)))
            sj[lanes(n), L : 2 * L] = jnp.where(lane < 6, ext, 0.0).astype(BF)
            return 0

        lax.fori_loop(0, G, body, 0)

    def aug_i(h):
        W = 512
        line = lax.broadcasted_iota(jnp.int32, (16, W), 0)

        def body(n, _):
            d = pl.ds(pl.multiple_of(n * W, W), W)
            v = si[h, 0:L, d].astype(F32)
            hi, mid, lo = split3(-0.5 * jnp.sum(v * v, axis=0, keepdims=True))
            ext = jnp.where(line == 3, hi, jnp.where(line == 4, mid, jnp.where(line == 5, lo, 1.0)))
            si[h, L : L + 16, d] = jnp.where(line < 6, ext, 0.0).astype(BF)
            return 0

        lax.fori_loop(0, HALF // W, body, 0)

    def build(h):
        M, W = 1024, 512

        def body(n, _):
            d = pl.ds(pl.multiple_of(n * W, W), W)
            pts = si[h, :, d]
            for m in range(HALF // M):
                e = slice(m * M, (m + 1) * M)
                neg = jnp.dot(sj[e, :], pts, preferred_element_type=F32)
                tile[h, e, d] = jnp.exp(jnp.minimum(neg, 0.0)).astype(BF)
            return 0

        lax.fori_loop(0, HALF // W, body, 0)

    recv_wait(3)
    aug_j()
    recv_wait(2)
    send(6, si.at[0, pl.ds(0, L)], si.at[1, pl.ds(0, L)], twin)
    expect(6, si.at[0, pl.ds(0, L)])
    aug_i(0)
    build(0)
    recv_wait(5)
    half = corr.at[:, half_of(core)]
    send(7, half, half, twin)
    expect(7, half)

    def apply(c):
        return lax.dot_general(
            corr[:, half_of(c)], basis[:, half_of(c)], (((1,), (1,)), ((), ())),
            preferred_element_type=F32,
        )

    pre = r + apply(core)
    d40[...] = zero
    d40[0:RHS, :] = prev[...]
    rz_row = jnp.concatenate([rz[...], jnp.ones((1, L - RHS), F32)], axis=1)
    rz_col = jnp.where(cid < RHS, to_col(rz_row), 1.0)
    recv_wait(7)
    pre = pre + apply(other)
    tail = corr[32:ROWS, 0:L].astype(F32)
    for g in range(1, 2 * G):
        tail = tail + corr[32:ROWS, g * L : (g + 1) * L].astype(F32)
    tid = lax.broadcasted_iota(jnp.int32, (8, L), 0)
    keep = (tid >= INNER - 32) & (tid < INNER - 29)
    inner = jnp.sum(jnp.where(keep, tail, 0.0), axis=0, keepdims=True)
    inner_col = to_col(inner + norm_all)
    beta = inner_col / rz_col
    direction = jnp.where(rid < RHS, pre + beta * d40[...], 0.0)
    d40[...] = direction
    d_own[...] = direction.astype(BF)

    def send4(dev, g):
        send(8, d_own, dj.at[:, lanes(g2)], dev)

    def send5(dev, g):
        send(9, d_own, di.at[:, lanes(g1)], dev)

    each(dev2, send4)
    each(dev1, send5)
    expect(8, dj.at[:, pl.ds(0, HALF - L)])
    expect(9, di.at[:, pl.ds(0, HALF - L)])
    dj[:, lanes(g2)] = d_own[...]
    di[:, lanes(g1)] = d_own[...]
    pre_out[...] = pre[0:RHS, :]
    beta_out[...] = jnp.broadcast_to(beta, (ROWS, L))[0:RHS, :]
    own_curv = NOISE * jnp.sum(direction * direction, axis=1, keepdims=True)

    recv_wait(6)
    aug_i(1)
    build(1)
    recv_wait(8)

    def image(h, out):
        W = 1024
        for n in range(HALF // W):
            d = slice(n * W, (n + 1) * W)
            out[:, d] = jnp.dot(dj[...], tile[h, :, d], preferred_element_type=F32).astype(out.dtype)

    image(1, im_send)
    send(10, im_send, im_recv, twin)
    expect(10, im_send)
    image(0, im_own)
    recv_wait(9)
    recv_wait(10)
    curv = zero
    for g in range(G):
        d = slice(g * L, (g + 1) * L)
        v = im_own[:, d] + im_recv[:, d].astype(F32)
        im_own[:, d] = v
        curv = curv + v * di[:, d].astype(F32)
    curv = to_row(jnp.sum(curv, axis=1, keepdims=True) + own_curv)
    curv_in = put(zero, NORM, curv)
    for g in range(G):
        d = slice(g * L, (g + 1) * L)
        e5_send[:, d] = (im_own[:, d] + curv_in).astype(BF)

    def send6(dev, g):
        send(11, e5_send.at[:, lanes(g)], e5.at[g1], dev)

    each(dev1, send6)
    expect(11, e5.at[pl.ds(0, G - 1)])
    e5[g1] = e5_send[:, lanes(g1)]
    recv_wait(11)
    acc = total(e5)
    c2_send[...] = take(acc, NORM)

    def send7(dev, g):
        send(12, c2_send, c2.at[g2], dev)

    each(dev2, send7)
    expect(12, c2.at[pl.ds(0, G - 1)])
    c2[g2] = c2_send[...]
    img_out[...] = (acc + NOISE * d40[...])[0:RHS, :]
    recv_wait(12)
    c3_send[...] = jnp.sum(c2[...], axis=0)
    send(13, c3_send, c3, twin)
    expect(13, c3_send)
    recv_wait(13)
    curv_col = jnp.where(cid < RHS, to_col(c3_send[...] + c3[...]), 1.0)
    alpha = inner_col / curv_col
    alpha_out[...] = jnp.broadcast_to(alpha, (ROWS, L))[0:RHS, :]
    drain()


def solution(mesh):
    axes = ("row", "col")
    pts = P(None, axes)
    placed = (pts, P(), P(axes, None), P(), pts, pts, pts, P())

    def step(points, inv_scale, basis, shrink, sol, res, prev, rz):
        rank = basis.shape[1]
        out = jax.ShapeDtypeStruct((RHS, L), F32)
        v = pl.BlockSpec(memory_space=pltpu.VMEM)
        pre, beta, alpha, img = pl.pallas_call(
            kernel,
            out_shape=(out,) * 4,
            in_specs=[v, v, pl.BlockSpec(memory_space=pl.ANY), v, v, v, v],
            out_specs=(v,) * 4,
            scratch_shapes=[
                pltpu.VMEM((L, rank), BF),
                pltpu.VMEM((ROWS, L), F32),
                pltpu.VMEM((L, L), BF),
                pltpu.VMEM((L, L), BF),
                pltpu.VMEM((2, 2 * L, HALF), BF),
                pltpu.VMEM((HALF, 2 * L), BF),
                pltpu.VMEM((2, HALF, HALF), BF),
                pltpu.VMEM((ROWS, HALF), BF),
                pltpu.VMEM((ROWS, HALF), BF),
                pltpu.VMEM((ROWS, HALF), BF),
                pltpu.VMEM((G, ROWS, L), BF),
                pltpu.VMEM((ROWS, L), BF),
                pltpu.VMEM((G, ROWS, L), BF),
                pltpu.VMEM((ROWS, L), BF),
                pltpu.VMEM((ROWS, rank), BF),
                pltpu.VMEM((ROWS, L), F32),
                pltpu.VMEM((ROWS, L), BF),
                pltpu.VMEM((ROWS, HALF), BF),
                pltpu.VMEM((ROWS, HALF), BF),
                pltpu.VMEM((ROWS, HALF), BF),
                pltpu.VMEM((ROWS, HALF), BF),
                pltpu.VMEM((ROWS, HALF), F32),
                pltpu.VMEM((ROWS, HALF), BF),
                pltpu.VMEM((G, ROWS, L), BF),
                pltpu.VMEM((1, L), F32),
                pltpu.VMEM((G, 1, L), F32),
                pltpu.VMEM((1, L), F32),
                pltpu.VMEM((1, L), F32),
                pltpu.SemaphoreType.DMA,
                pltpu.SemaphoreType.DMA((14,)),
                pltpu.SemaphoreType.DMA((14,)),
            ],
            compiler_params=pltpu.CompilerParams(
                collective_id=0, has_side_effects=True, vmem_limit_bytes=62 * 1024 * 1024
            ),
            name="cg_step",
        )(
            points, inv_scale.reshape(1, L), basis, shrink.reshape(rank // L, L),
            res, prev, rz.reshape(1, RHS),
        )
        direction = pre + beta * prev
        return sol + alpha * direction, res - alpha * img, direction

    return jax.shard_map(
        step, mesh=mesh, in_specs=placed, out_specs=(pts, pts, pts), check_vma=False
    )
```

time: 740 us -> 69.6 us (0.09)
  waiting for transfers between devices: 467 us -> 0 us
  blocking collectives: 236 us -> 0 us
  Pallas kernels: 0 us -> 67.2 us
  between operations: 15.6 us -> 0.69 us
  matrix products: 14.4 us -> 0 us
    psum x1 -> x0, waiting for transfers between devices: 257 us -> none  [local(): projected = lax.psum(local_proj, ('row', 'col'))]
    unnamed x4 -> x0, waiting for transfers between devices: 211 us -> none
    psum x2 -> x0, blocking collectives: 198 us -> none  [the longest x1 101 us: local(): curvature = lax.psum(jnp.sum(direction * image, axis=1), ('row', 'col'))]
    pallas_call x0 -> x1, Pallas kernels: none -> 67.2 us  [step(): pl.pallas_call(kernel, out_shape=(out,) * 4, in_specs=[v, v, pl.BlockSpec...]
    all_gather x2 -> x0, blocking collectives: 38 us -> none  [the longest x1 22.7 us: local(): column_pts = lax.all_gather(scaled, 'row', axis=1, tiled=True)]
    dot_general x6 -> x0, matrix products: 14.4 us -> none  [the longest x4 10.9 us: local(): jnp.dot(direction_piece, tile, preferred_element_type=jnp.float32)]
  transfers between devices with their start and end apart: 3 -> 0, of which waited for: 2 -> 0; matrix products, arithmetic and copies ran while one was open for 0% -> 0% of each run, Pallas kernels for 0% -> 0%
where the time goes in v2:
time: 69.6 us; the launch traced here: 69.3 us
  Pallas kernels  67.2 us (97%)
  other arithmetic  1.41 us (2%)
    pallas_call x1, Pallas kernels, step(): pl.pallas_call(kernel, out_shape=(out,) * 4, in_specs=[v, v, pl.BlockSpec...  67.2 us
    add x1, other arithmetic, step(): return (sol + alpha * direction, res - alpha * img, direction)  1.41 us

profile of v2, /device:TPU:1, one launch (start us, length us, event | category | flops | bytes accessed | tf_op | source)
XLA Modules:
  0.0 69.3 jit_solution(8636037000076194907)
XLA Ops:
  0.6 0.0 copy-start
  0.6 0.0 copy-start.1
  0.7 0.0 copy-start.2
  0.7 67.2 %cg_step.1 = (f32[33,128]{1,0:T(8,128)}, f32[33,128]{1,0:T(8,128)}, f32[33,128]{1,0:T(8,128)}, f32[33,128]{1,0:T(8,128)}) custom-call(bf16[128,128]{1,0:T(8,128)(2,1)} %points.1, f32[1,128]{1,0:T(1,128)} %bitcast.4, bf16[128,4096]{1,0:T(8,128)(2,1)} %basis_hbm.1, f32[32,128]{1,0:T(8,128)} %bitcast.3, f32[33,128]{1,0:T(8,128)} %res.1, f32[33,128]{1,0:T(8,128)} %prev.1, ...), custom_call_target="tpu_custom_call" | custom-call | tf_op jit(solution)/shard_map/cg_step/pallas_call | solution.py:375
  67.8 0.0 copy-done
  67.8 0.0 copy-done.1
  67.9 0.0 copy-done.2
  67.9 1.4 %multiply_add_fusion = (f32[33,128]{1,0:T(8,128)}, f32[33,128]{1,0:T(8,128)}, f32[33,128]{1,0:T(8,128)}) fusion(f32[33,128]{1,0:T(8,128)S(1)} %copy-done.2, f32[33,128]{1,0:T(8,128)} %get-tuple-element.7, f32[33,128]{1,0:T(8,128)} %get-tuple-element.8, f32[33,128]{1,0:T(8,128)} %get-tuple-element.9, f32[33,128]{1,0:T(8,128)S(1)} %copy-done.1, ...), kind=kLoop, calls=%fused_computation.1 | loop fusion | flops 25344 | bytes 168960 | tf_op jit(solution)/shard_map/add | solution.py:422
Async XLA Ops:
  0.6 67.2 %copy-start = (f32[33,128]{1,0:T(8,128)S(1)}, f32[33,128]{1,0:T(8,128)}, u32[]{:S(2)}) copy-start(f32[33,128]{1,0:T(8,128)} %res.1) | copy-start | bytes 50692
  0.6 67.2 %copy-start.1 = (f32[33,128]{1,0:T(8,128)S(1)}, f32[33,128]{1,0:T(8,128)}, u32[]{:S(2)}) copy-start(f32[33,128]{1,0:T(8,128)} %prev.1) | copy-start | bytes 50692
  0.7 67.2 %copy-start.2 = (f32[33,128]{1,0:T(8,128)S(1)}, f32[33,128]{1,0:T(8,128)}, u32[]{:S(2)}) copy-start(f32[33,128]{1,0:T(8,128)} %param.12) | copy-start | bytes 50692

commit v3 on v2

--- a/solution.py
+++ b/solution.py
@@ -29,7 +29,7 @@
     pre_out, beta_out, alpha_out, img_out,
     basis, r40, s_own, st_own, si, sj, tile,
     p_send, p_recv, p_half, e1, e2_send, e2, corr_own, corr, d40, d_own, dj, di,
-    im_send, im_recv, im_own, e5_send, e5, c2_send, c2, c3_send, c3,
+    im_send, im_recv, im_own, e5_send, e5, c2_send, c2,
     basis_sem, ssem, rsem,
 ):
     row = lax.axis_index("row")
@@ -40,7 +40,7 @@
     x = col % 4
     xa = x // 2
     xb = ((x + 1) // 2) % 2
-    g1 = z * 2 + xb
+    g1 = xb * 8 + z
     g2 = y * 2 + xa
     other = 1 - core
     twin = (y * 2 + other, col)
@@ -51,12 +51,12 @@
     def dev1(t, flip):
         zz = (z + far(t)) % 8
         b = (xb + flip) % 2
-        return (row, zz * 4 + 3 * xa + b - 2 * xa * b), zz * 2 + b
-
-    def dev2(t, flip):
+        return (row, zz * 4 + 3 * xa + b - 2 * xa * b), b * 8 + zz
+
+    def dev2(t, flip, c=core):
         yy = (y + far(t)) % 8
         a = (xa + flip) % 2
-        return (yy * 2 + core, z * 4 + 3 * a + xb - 2 * a * xb), yy * 2 + a
+        return (yy * 2 + c, z * 4 + 3 * a + xb - 2 * a * xb), 2 * t + 1 - flip
 
     def each(dev, fn, lo=0, hi=8):
         def body(t, _):
@@ -109,7 +109,7 @@
     s_own[...] = scaled
     st_own[...] = scaled.astype(F32).T.astype(BF)
     si[0, 0:L, lanes(g1)] = s_own[...]
-    sj[lanes(g2), 0:L] = st_own[...]
+    sj[HALF - L : HALF, 0:L] = st_own[...]
     for h in range(2):
         si[h, L : 2 * L, :] = jnp.zeros((L, HALF), BF)
 
@@ -157,15 +157,19 @@
     expect(0, p_send)
 
     def send_j(dev, g):
-        send(3, st_own, sj.at[lanes(g2), pl.ds(0, L)], dev)
-
-    def send_i(dev, g):
-        send(2, s_own, si.at[0, pl.ds(0, L), lanes(g1)], dev)
+        send(3, st_own, sj.at[lanes(g), pl.ds(0, L)], dev)
+
+    def send_i():
+        def body(t, _):
+            send(2, s_own, si.at[0, pl.ds(0, L), lanes(g1)], dev1(t, 0)[0])
+            return 0
+
+        lax.fori_loop(0, 7, body, 0)
+        expect(2, si.at[0, pl.ds(0, L), pl.ds(0, 7 * L)])
 
     each(dev2, send_j)
     expect(3, sj.at[pl.ds(0, HALF - L), pl.ds(0, L)])
-    each(dev1, send_i, 5, 8)
-    expect(2, si.at[0, pl.ds(0, L), pl.ds(0, HALF - L)])
+    send_i()
 
     recv_wait(0)
     norm_in = put(zero, NORM, norm + take(p_recv[:, 0:L].astype(F32), NORM))
@@ -196,7 +200,10 @@
 
     each(dev2, send2)
     expect(4, e2.at[pl.ds(0, G - 1)])
-    each(dev1, send_i, 0, 5)
+    recv_wait(2)
+    relay = si.at[0, pl.ds(0, L), pl.ds(pl.multiple_of(xb * 8 * L, 8 * L), 8 * L)]
+    send(14, relay, relay, dev1(7, 1)[0])
+    expect(14, relay)
     e2[g2] = e2_send[...]
     recv_wait(4)
     acc = total(e2)
@@ -255,7 +262,7 @@
 
     recv_wait(3)
     aug_j()
-    recv_wait(2)
+    recv_wait(14)
     send(6, si.at[0, pl.ds(0, L)], si.at[1, pl.ds(0, L)], twin)
     expect(6, si.at[0, pl.ds(0, L)])
     aug_i(0)
@@ -291,7 +298,7 @@
     d_own[...] = direction.astype(BF)
 
     def send4(dev, g):
-        send(8, d_own, dj.at[:, lanes(g2)], dev)
+        send(8, d_own, dj.at[:, lanes(g)], dev)
 
     def send5(dev, g):
         send(9, d_own, di.at[:, lanes(g1)], dev)
@@ -300,7 +307,7 @@
     each(dev1, send5)
     expect(8, dj.at[:, pl.ds(0, HALF - L)])
     expect(9, di.at[:, pl.ds(0, HALF - L)])
-    dj[:, lanes(g2)] = d_own[...]
+    dj[:, HALF - L : HALF] = d_own[...]
     di[:, lanes(g1)] = d_own[...]
     pre_out[...] = pre[0:RHS, :]
     beta_out[...] = jnp.broadcast_to(beta, (ROWS, L))[0:RHS, :]
@@ -342,22 +349,31 @@
     expect(11, e5.at[pl.ds(0, G - 1)])
     e5[g1] = e5_send[:, lanes(g1)]
     recv_wait(11)
-    acc = total(e5)
-    c2_send[...] = take(acc, NORM)
-
-    def send7(dev, g):
-        send(12, c2_send, c2.at[g2], dev)
-
-    each(dev2, send7)
-    expect(12, c2.at[pl.ds(0, G - 1)])
-    c2[g2] = c2_send[...]
-    img_out[...] = (acc + NOISE * d40[...])[0:RHS, :]
+    tail = e5[0, 32:ROWS, :].astype(F32)
+    for g in range(1, G):
+        tail = tail + e5[g, 32:ROWS, :].astype(F32)
+    keep = (tid >= NORM - 32) & (tid < NORM - 29)
+    c2_send[...] = jnp.sum(jnp.where(keep, tail, 0.0), axis=0, keepdims=True)
+    mine = c2.at[core * G + g2]
+
+    def send7(dev, _):
+        send(12, c2_send, mine, dev)
+
+    def both(t, _):
+        for flip in (1, 0):
+            for c in (core, other):
+                send7(dev2(t, flip, c)[0], 0)
+        return 0
+
+    lax.fori_loop(0, 7, both, 0)
+    send7(dev2(7, 1, core)[0], 0)
+    send7(dev2(7, 1, other)[0], 0)
+    send7(twin, 0)
+    expect(12, c2.at[pl.ds(0, 2 * G - 1)])
+    c2[core * G + g2] = c2_send[...]
+    img_out[...] = (total(e5) + NOISE * d40[...])[0:RHS, :]
     recv_wait(12)
-    c3_send[...] = jnp.sum(c2[...], axis=0)
-    send(13, c3_send, c3, twin)
-    expect(13, c3_send)
-    recv_wait(13)
-    curv_col = jnp.where(cid < RHS, to_col(c3_send[...] + c3[...]), 1.0)
+    curv_col = jnp.where(cid < RHS, to_col(jnp.sum(c2[...], axis=0)), 1.0)
     alpha = inner_col / curv_col
     alpha_out[...] = jnp.broadcast_to(alpha, (ROWS, L))[0:RHS, :]
     drain()
@@ -403,12 +419,10 @@
                 pltpu.VMEM((ROWS, HALF), BF),
                 pltpu.VMEM((G, ROWS, L), BF),
                 pltpu.VMEM((1, L), F32),
-                pltpu.VMEM((G, 1, L), F32),
-                pltpu.VMEM((1, L), F32),
-                pltpu.VMEM((1, L), F32),
+                pltpu.VMEM((2 * G, 1, L), F32),
                 pltpu.SemaphoreType.DMA,
-                pltpu.SemaphoreType.DMA((14,)),
-                pltpu.SemaphoreType.DMA((14,)),
+                pltpu.SemaphoreType.DMA((15,)),
+                pltpu.SemaphoreType.DMA((15,)),
             ],
             compiler_params=pltpu.CompilerParams(
                 collective_id=0, has_side_effects=True, vmem_limit_bytes=62 * 1024 * 1024

time: 69.6 us -> 66.9 us (0.961)
  Pallas kernels: 67.2 us -> 64.4 us
    pallas_call x1, Pallas kernels: 67.2 us -> 64.4 us  [step(): pl.pallas_call(kernel, out_shape=(out,) * 4, in_specs=[v, v, pl.BlockSpec...]
where the time goes in v3:
time: 66.9 us; the launch traced here: 66.5 us
  Pallas kernels  64.4 us (96%)
  other arithmetic  1.41 us (2%)
  between operations  0.69 us (1%)
    pallas_call x1, Pallas kernels, step(): pl.pallas_call(kernel, out_shape=(out,) * 4, in_specs=[v, v, pl.BlockSpec...  64.4 us
    add x1, other arithmetic, step(): return (sol + alpha * direction, res - alpha * img, direction)  1.41 us

profile of v3, /device:TPU:1, one launch (start us, length us, event | category | flops | bytes accessed | tf_op | source)
XLA Modules:
  0.0 66.5 jit_solution(12400176696605172145)
XLA Ops:
  0.6 0.0 copy-start
  0.6 0.0 copy-start.1
  0.7 0.0 copy-start.2
  0.7 64.4 %cg_step.1 = (f32[33,128]{1,0:T(8,128)}, f32[33,128]{1,0:T(8,128)}, f32[33,128]{1,0:T(8,128)}, f32[33,128]{1,0:T(8,128)}) custom-call(bf16[128,128]{1,0:T(8,128)(2,1)} %points.1, f32[1,128]{1,0:T(1,128)} %bitcast.4, bf16[128,4096]{1,0:T(8,128)(2,1)} %basis_hbm.1, f32[32,128]{1,0:T(8,128)} %bitcast.3, f32[33,128]{1,0:T(8,128)} %res.1, f32[33,128]{1,0:T(8,128)} %prev.1, ...), custom_call_target="tpu_custom_call" | custom-call | tf_op jit(solution)/shard_map/cg_step/pallas_call | solution.py:391
  65.1 0.0 copy-done
  65.1 0.0 copy-done.1
  65.1 0.0 copy-done.2
  65.1 1.4 %multiply_add_fusion = (f32[33,128]{1,0:T(8,128)}, f32[33,128]{1,0:T(8,128)}, f32[33,128]{1,0:T(8,128)}) fusion(f32[33,128]{1,0:T(8,128)S(1)} %copy-done.2, f32[33,128]{1,0:T(8,128)} %get-tuple-element.7, f32[33,128]{1,0:T(8,128)} %get-tuple-element.8, f32[33,128]{1,0:T(8,128)} %get-tuple-element.9, f32[33,128]{1,0:T(8,128)S(1)} %copy-done.1, ...), kind=kLoop, calls=%fused_computation.1 | loop fusion | flops 25344 | bytes 168960 | tf_op jit(solution)/shard_map/add | solution.py:436
Async XLA Ops:
  0.6 64.5 %copy-start = (f32[33,128]{1,0:T(8,128)S(1)}, f32[33,128]{1,0:T(8,128)}, u32[]{:S(2)}) copy-start(f32[33,128]{1,0:T(8,128)} %res.1) | copy-start | bytes 50692
  0.6 64.5 %copy-start.1 = (f32[33,128]{1,0:T(8,128)S(1)}, f32[33,128]{1,0:T(8,128)}, u32[]{:S(2)}) copy-start(f32[33,128]{1,0:T(8,128)} %prev.1) | copy-start | bytes 50692
  0.7 64.5 %copy-start.2 = (f32[33,128]{1,0:T(8,128)S(1)}, f32[33,128]{1,0:T(8,128)}, u32[]{:S(2)}) copy-start(f32[33,128]{1,0:T(8,128)} %param.12) | copy-start | bytes 50692

commit v4 on v3

--- a/solution.py
+++ b/solution.py
@@ -12,6 +12,7 @@
 G = 16
 L = 128
 HALF = G * L
+PART = HALF // 2
 RHS = 33
 ROWS = 40
 NORM = 33
@@ -56,7 +57,21 @@
     def dev2(t, flip, c=core):
         yy = (y + far(t)) % 8
         a = (xa + flip) % 2
-        return (yy * 2 + c, z * 4 + 3 * a + xb - 2 * a * xb), 2 * t + 1 - flip
+        return (yy * 2 + c, z * 4 + 3 * a + xb - 2 * a * xb), flip * 8 + t
+
+    def ordered(u, v):
+        def dev(t, flip):
+            zz = (z + far(t) * u) % 8
+            yy = (y + far(t) * v) % 8
+            b = (xb + flip * u) % 2
+            a = (xa + flip * v) % 2
+            place = (yy * 2 + core, zz * 4 + 3 * a + b - 2 * a * b)
+            return place, (b * 8 + zz) * u + (a * 8 + yy) * v
+
+        return dev, (xb * 8 + z) * u + (xa * 8 + y) * v
+
+    dev_a, g_a = ordered(other, core)
+    dev_b, g_b = ordered(core, other)
 
     def each(dev, fn, lo=0, hi=8):
         def body(t, _):
@@ -109,7 +124,7 @@
     s_own[...] = scaled
     st_own[...] = scaled.astype(F32).T.astype(BF)
     si[0, 0:L, lanes(g1)] = s_own[...]
-    sj[HALF - L : HALF, 0:L] = st_own[...]
+    sj[7 * L : 8 * L, 0:L] = st_own[...]
     for h in range(2):
         si[h, L : 2 * L, :] = jnp.zeros((L, HALF), BF)
 
@@ -156,21 +171,14 @@
     send(0, p_send, p_recv, twin)
     expect(0, p_send)
 
-    def send_j(dev, g):
+    def send_pts(t, _):
+        dev, g = dev2(t, 0)
         send(3, st_own, sj.at[lanes(g), pl.ds(0, L)], dev)
-
-    def send_i():
-        def body(t, _):
-            send(2, s_own, si.at[0, pl.ds(0, L), lanes(g1)], dev1(t, 0)[0])
-            return 0
-
-        lax.fori_loop(0, 7, body, 0)
-        expect(2, si.at[0, pl.ds(0, L), pl.ds(0, 7 * L)])
-
-    each(dev2, send_j)
-    expect(3, sj.at[pl.ds(0, HALF - L), pl.ds(0, L)])
-    send_i()
-
+        send(2, s_own, si.at[0, pl.ds(0, L), lanes(g1)], dev1(t, 0)[0])
+        return 0
+
+    expect(3, sj.at[pl.ds(0, 7 * L), pl.ds(0, L)])
+    expect(2, si.at[0, pl.ds(0, L), pl.ds(0, 7 * L)])
     recv_wait(0)
     norm_in = put(zero, NORM, norm + take(p_recv[:, 0:L].astype(F32), NORM))
     for g in range(G):
@@ -179,11 +187,12 @@
         p_half[:, d] = jnp.where(rid < RHS, v, norm_in).astype(BF)
 
     def send1(dev, g):
-        send(1, p_half.at[:, lanes(g)], e1.at[g1], dev)
-
-    each(dev1, send1)
+        send(1, p_half.at[:, lanes(g)], e1.at[g_a], dev)
+
+    each(dev_a, send1)
     expect(1, e1.at[pl.ds(0, G - 1)])
-    e1[g1] = p_half[:, lanes(g1)]
+    lax.fori_loop(0, 3, send_pts, 0)
+    e1[g_a] = p_half[:, lanes(g_a)]
 
     def total(ref):
         acc = ref[0].astype(F32)
@@ -196,33 +205,30 @@
     e2_send[...] = put(acc, NORM, take(acc, NORM)).astype(BF)
 
     def send2(dev, g):
-        send(4, e2_send, e2.at[g2], dev)
-
-    each(dev2, send2)
+        send(4, e2_send, e2.at[g_b], dev)
+
+    each(dev_b, send2)
     expect(4, e2.at[pl.ds(0, G - 1)])
-    recv_wait(2)
-    relay = si.at[0, pl.ds(0, L), pl.ds(pl.multiple_of(xb * 8 * L, 8 * L), 8 * L)]
-    send(14, relay, relay, dev1(7, 1)[0])
-    expect(14, relay)
-    e2[g2] = e2_send[...]
+    lax.fori_loop(3, 7, send_pts, 0)
+    e2[g_b] = e2_send[...]
     recv_wait(4)
     acc = total(e2)
     norm_all = take(acc, NORM)
     proj = jnp.where(rid < RHS, acc, 0.0)
-    cor = ((shrink[pl.ds(core * G + g1, 1), :] - 1.0) * proj).astype(BF).astype(F32)
+    cor = ((shrink[pl.ds(core * G + g_a, 1), :] - 1.0) * proj).astype(BF).astype(F32)
     inner = to_row(jnp.sum(cor * proj, axis=1, keepdims=True))
     corr_own[...] = put(cor, INNER, inner).astype(BF)
 
     def send3(dev, g):
-        send(5, corr_own, corr.at[:, lanes(core * G + g1)], dev)
-
-    each(dev1, send3)
+        send(5, corr_own, corr.at[:, lanes(core * G + g_a)], dev)
+
+    each(dev_a, send3)
     expect(5, corr.at[:, pl.ds(0, HALF - L)])
-    corr[:, lanes(core * G + g1)] = corr_own[...]
+    corr[:, lanes(core * G + g_a)] = corr_own[...]
 
     lane = lax.broadcasted_iota(jnp.int32, (L, L), 1)
 
-    def aug_j():
+    def aug_j(lo, hi):
         def body(n, _):
             v = sj[lanes(n), 0:L].astype(F32)
             hi, mid, lo = split3(jnp.broadcast_to(-0.5 * jnp.sum(v * v, axis=1, keepdims=True), (L, L)))
@@ -230,43 +236,52 @@
             sj[lanes(n), L : 2 * L] = jnp.where(lane < 6, ext, 0.0).astype(BF)
             return 0
 
-        lax.fori_loop(0, G, body, 0)
-
-    def aug_i(h):
+        lax.fori_loop(lo, hi, body, 0)
+
+    def aug_i(h, off):
         W = 512
         line = lax.broadcasted_iota(jnp.int32, (16, W), 0)
 
         def body(n, _):
-            d = pl.ds(pl.multiple_of(n * W, W), W)
+            d = pl.ds(pl.multiple_of(off + n * W, W), W)
             v = si[h, 0:L, d].astype(F32)
             hi, mid, lo = split3(-0.5 * jnp.sum(v * v, axis=0, keepdims=True))
             ext = jnp.where(line == 3, hi, jnp.where(line == 4, mid, jnp.where(line == 5, lo, 1.0)))
             si[h, L : L + 16, d] = jnp.where(line < 6, ext, 0.0).astype(BF)
             return 0
 
-        lax.fori_loop(0, HALF // W, body, 0)
-
-    def build(h):
-        M, W = 1024, 512
-
-        def body(n, _):
-            d = pl.ds(pl.multiple_of(n * W, W), W)
-            pts = si[h, :, d]
-            for m in range(HALF // M):
-                e = slice(m * M, (m + 1) * M)
-                neg = jnp.dot(sj[e, :], pts, preferred_element_type=F32)
-                tile[h, e, d] = jnp.exp(jnp.minimum(neg, 0.0)).astype(BF)
+        lax.fori_loop(0, PART // W, body, 0)
+
+    def build(h, off, lo, hi):
+        W = 512
+
+        def body(k, _):
+            e = pl.ds(pl.multiple_of((k // 2) * PART, PART), PART)
+            d = pl.ds(pl.multiple_of(off + (k % 2) * W, W), W)
+            neg = jnp.dot(sj[e, :], si[h, :, d], preferred_element_type=F32)
+            tile[h, e, d] = jnp.exp(jnp.minimum(neg, 0.0)).astype(BF)
             return 0
 
-        lax.fori_loop(0, HALF // W, body, 0)
+        lax.fori_loop(2 * lo, 2 * hi, body, 0)
+
+    mine = xb * PART
+    rest = (1 - xb) * PART
+
+    def block(h, off):
+        return si.at[h, pl.ds(0, L), pl.ds(pl.multiple_of(off, PART), PART)]
 
     recv_wait(3)
-    aug_j()
-    recv_wait(14)
-    send(6, si.at[0, pl.ds(0, L)], si.at[1, pl.ds(0, L)], twin)
-    expect(6, si.at[0, pl.ds(0, L)])
-    aug_i(0)
-    build(0)
+    dst = sj.at[pl.ds(PART, PART), pl.ds(0, L)]
+    send(13, sj.at[pl.ds(0, PART), pl.ds(0, L)], dst, dev2(7, 1)[0])
+    expect(13, dst)
+    recv_wait(2)
+    send(14, block(0, mine), block(0, mine), dev1(7, 1)[0])
+    expect(14, block(0, mine))
+    send(6, block(0, mine), block(1, mine), twin)
+    expect(6, block(1, mine))
+    aug_j(0, 8)
+    aug_i(0, mine)
+    build(0, mine, 0, 1)
     recv_wait(5)
     half = corr.at[:, half_of(core)]
     send(7, half, half, twin)
@@ -307,15 +322,27 @@
     each(dev1, send5)
     expect(8, dj.at[:, pl.ds(0, HALF - L)])
     expect(9, di.at[:, pl.ds(0, HALF - L)])
-    dj[:, HALF - L : HALF] = d_own[...]
+    dj[:, 7 * L : 8 * L] = d_own[...]
     di[:, lanes(g1)] = d_own[...]
     pre_out[...] = pre[0:RHS, :]
     beta_out[...] = jnp.broadcast_to(beta, (ROWS, L))[0:RHS, :]
     own_curv = NOISE * jnp.sum(direction * direction, axis=1, keepdims=True)
 
+    recv_wait(14)
+    send(15, block(0, rest), block(1, rest), twin)
+    expect(15, block(1, rest))
     recv_wait(6)
-    aug_i(1)
-    build(1)
+    aug_i(1, mine)
+    build(1, mine, 0, 1)
+    recv_wait(13)
+    aug_j(8, G)
+    build(0, mine, 1, 2)
+    build(1, mine, 1, 2)
+    aug_i(0, rest)
+    build(0, rest, 0, 2)
+    recv_wait(15)
+    aug_i(1, rest)
+    build(1, rest, 0, 2)
     recv_wait(8)
 
     def image(h, out):
@@ -354,10 +381,10 @@
         tail = tail + e5[g, 32:ROWS, :].astype(F32)
     keep = (tid >= NORM - 32) & (tid < NORM - 29)
     c2_send[...] = jnp.sum(jnp.where(keep, tail, 0.0), axis=0, keepdims=True)
-    mine = c2.at[core * G + g2]
+    slot = c2.at[core * G + g2]
 
     def send7(dev, _):
-        send(12, c2_send, mine, dev)
+        send(12, c2_send, slot, dev)
 
     def both(t, _):
         for flip in (1, 0):
@@ -421,8 +448,8 @@
                 pltpu.VMEM((1, L), F32),
                 pltpu.VMEM((2 * G, 1, L), F32),
                 pltpu.SemaphoreType.DMA,
-                pltpu.SemaphoreType.DMA((15,)),
-                pltpu.SemaphoreType.DMA((15,)),
+                pltpu.SemaphoreType.DMA((16,)),
+                pltpu.SemaphoreType.DMA((16,)),
             ],
             compiler_params=pltpu.CompilerParams(
                 collective_id=0, has_side_effects=True, vmem_limit_bytes=62 * 1024 * 1024

time: 66.9 us -> 65.2 us (0.975)
  Pallas kernels: 64.4 us -> 62.7 us
    pallas_call x1, Pallas kernels: 64.4 us -> 62.7 us  [step(): pl.pallas_call(kernel, out_shape=(out,) * 4, in_specs=[v, v, pl.BlockSpec...]
where the time goes in v4:
time: 65.2 us; the launch traced here: 64.8 us
  Pallas kernels  62.7 us (96%)
  other arithmetic  1.41 us (2%)
  between operations  0.69 us (1%)
    pallas_call x1, Pallas kernels, step(): pl.pallas_call(kernel, out_shape=(out,) * 4, in_specs=[v, v, pl.BlockSpec...  62.7 us
    add x1, other arithmetic, step(): return (sol + alpha * direction, res - alpha * img, direction)  1.41 us

profile of v4, /device:TPU:1, one launch (start us, length us, event | category | flops | bytes accessed | tf_op | source)
XLA Modules:
  0.0 64.8 jit_solution(398086034639772355)
XLA Ops:
  0.6 0.0 copy-start
  0.6 0.0 copy-start.1
  0.7 0.0 copy-start.2
  0.7 62.7 %cg_step.1 = (f32[33,128]{1,0:T(8,128)}, f32[33,128]{1,0:T(8,128)}, f32[33,128]{1,0:T(8,128)}, f32[33,128]{1,0:T(8,128)}) custom-call(bf16[128,128]{1,0:T(8,128)(2,1)} %points.1, f32[1,128]{1,0:T(1,128)} %bitcast.4, bf16[128,4096]{1,0:T(8,128)(2,1)} %basis_hbm.1, f32[32,128]{1,0:T(8,128)} %bitcast.3, f32[33,128]{1,0:T(8,128)} %res.1, f32[33,128]{1,0:T(8,128)} %prev.1, ...), custom_call_target="tpu_custom_call" | custom-call | tf_op jit(solution)/shard_map/cg_step/pallas_call | solution.py:418
  63.4 0.0 copy-done
  63.4 0.0 copy-done.1
  63.4 0.0 copy-done.2
  63.4 1.4 %multiply_add_fusion = (f32[33,128]{1,0:T(8,128)}, f32[33,128]{1,0:T(8,128)}, f32[33,128]{1,0:T(8,128)}) fusion(f32[33,128]{1,0:T(8,128)S(1)} %copy-done.2, f32[33,128]{1,0:T(8,128)} %get-tuple-element.7, f32[33,128]{1,0:T(8,128)} %get-tuple-element.8, f32[33,128]{1,0:T(8,128)} %get-tuple-element.9, f32[33,128]{1,0:T(8,128)S(1)} %copy-done.1, ...), kind=kLoop, calls=%fused_computation.1 | loop fusion | flops 25344 | bytes 168960 | tf_op jit(solution)/shard_map/add | solution.py:463
Async XLA Ops:
  0.6 62.8 %copy-start = (f32[33,128]{1,0:T(8,128)S(1)}, f32[33,128]{1,0:T(8,128)}, u32[]{:S(2)}) copy-start(f32[33,128]{1,0:T(8,128)} %res.1) | copy-start | bytes 50692
  0.6 62.8 %copy-start.1 = (f32[33,128]{1,0:T(8,128)S(1)}, f32[33,128]{1,0:T(8,128)}, u32[]{:S(2)}) copy-start(f32[33,128]{1,0:T(8,128)} %prev.1) | copy-start | bytes 50692
  0.7 62.8 %copy-start.2 = (f32[33,128]{1,0:T(8,128)S(1)}, f32[33,128]{1,0:T(8,128)}, u32[]{:S(2)}) copy-start(f32[33,128]{1,0:T(8,128)} %param.12) | copy-start | bytes 50692

commit v5 on v4

--- a/solution.py
+++ b/solution.py
@@ -26,12 +26,12 @@
 
 
 def kernel(
-    points, inv_scale, basis_hbm, shrink, res, prev, rz,
+    points_h, inv_h, basis_hbm, shrink_h, res_h, prev_h, rz_h,
     pre_out, beta_out, alpha_out, img_out,
-    basis, r40, s_own, st_own, si, sj, tile,
+    points, inv_scale, shrink, res, prev, rz, basis, r40, s_own, st_own, si, sj, tile,
     p_send, p_recv, p_half, e1, e2_send, e2, corr_own, corr, d40, d_own, dj, di,
     im_send, im_recv, im_own, e5_send, e5, c2_send, c2,
-    basis_sem, ssem, rsem,
+    basis_sem, in_sem, ssem, rsem,
 ):
     row = lax.axis_index("row")
     col = lax.axis_index("col")
@@ -110,7 +110,17 @@
 
     bar = pltpu.get_barrier_semaphore()
     cp = pltpu.make_async_copy(basis_hbm, basis, basis_sem)
+    ins = [
+        pltpu.make_async_copy(a, b, in_sem.at[i])
+        for i, (a, b) in enumerate((
+            (res_h, res), (points_h, points), (inv_h, inv_scale),
+            (shrink_h, shrink), (prev_h, prev), (rz_h, rz),
+        ))
+    ]
+    ins[0].start()
     cp.start()
+    for c in ins[1:]:
+        c.start()
 
     def signal(dev, _):
         pl.semaphore_signal(bar, inc=1, device_id=dev, device_id_type=MESH)
@@ -119,6 +129,8 @@
     each(dev1, signal)
     each(dev2, signal)
 
+    for c in ins:
+        c.wait()
     inv_col = jnp.broadcast_to(inv_scale[...], (L, L)).T
     scaled = (points[...].astype(F32) * inv_col).astype(BF)
     s_own[...] = scaled
@@ -191,7 +203,7 @@
 
     each(dev_a, send1)
     expect(1, e1.at[pl.ds(0, G - 1)])
-    lax.fori_loop(0, 3, send_pts, 0)
+    lax.fori_loop(0, 7, send_pts, 0)
     e1[g_a] = p_half[:, lanes(g_a)]
 
     def total(ref):
@@ -209,61 +221,7 @@
 
     each(dev_b, send2)
     expect(4, e2.at[pl.ds(0, G - 1)])
-    lax.fori_loop(3, 7, send_pts, 0)
     e2[g_b] = e2_send[...]
-    recv_wait(4)
-    acc = total(e2)
-    norm_all = take(acc, NORM)
-    proj = jnp.where(rid < RHS, acc, 0.0)
-    cor = ((shrink[pl.ds(core * G + g_a, 1), :] - 1.0) * proj).astype(BF).astype(F32)
-    inner = to_row(jnp.sum(cor * proj, axis=1, keepdims=True))
-    corr_own[...] = put(cor, INNER, inner).astype(BF)
-
-    def send3(dev, g):
-        send(5, corr_own, corr.at[:, lanes(core * G + g_a)], dev)
-
-    each(dev_a, send3)
-    expect(5, corr.at[:, pl.ds(0, HALF - L)])
-    corr[:, lanes(core * G + g_a)] = corr_own[...]
-
-    lane = lax.broadcasted_iota(jnp.int32, (L, L), 1)
-
-    def aug_j(lo, hi):
-        def body(n, _):
-            v = sj[lanes(n), 0:L].astype(F32)
-            hi, mid, lo = split3(jnp.broadcast_to(-0.5 * jnp.sum(v * v, axis=1, keepdims=True), (L, L)))
-            ext = jnp.where(lane == 0, hi, jnp.where(lane == 1, mid, jnp.where(lane == 2, lo, 1.0)))
-            sj[lanes(n), L : 2 * L] = jnp.where(lane < 6, ext, 0.0).astype(BF)
-            return 0
-
-        lax.fori_loop(lo, hi, body, 0)
-
-    def aug_i(h, off):
-        W = 512
-        line = lax.broadcasted_iota(jnp.int32, (16, W), 0)
-
-        def body(n, _):
-            d = pl.ds(pl.multiple_of(off + n * W, W), W)
-            v = si[h, 0:L, d].astype(F32)
-            hi, mid, lo = split3(-0.5 * jnp.sum(v * v, axis=0, keepdims=True))
-            ext = jnp.where(line == 3, hi, jnp.where(line == 4, mid, jnp.where(line == 5, lo, 1.0)))
-            si[h, L : L + 16, d] = jnp.where(line < 6, ext, 0.0).astype(BF)
-            return 0
-
-        lax.fori_loop(0, PART // W, body, 0)
-
-    def build(h, off, lo, hi):
-        W = 512
-
-        def body(k, _):
-            e = pl.ds(pl.multiple_of((k // 2) * PART, PART), PART)
-            d = pl.ds(pl.multiple_of(off + (k % 2) * W, W), W)
-            neg = jnp.dot(sj[e, :], si[h, :, d], preferred_element_type=F32)
-            tile[h, e, d] = jnp.exp(jnp.minimum(neg, 0.0)).astype(BF)
-            return 0
-
-        lax.fori_loop(2 * lo, 2 * hi, body, 0)
-
     mine = xb * PART
     rest = (1 - xb) * PART
 
@@ -279,9 +237,65 @@
     expect(14, block(0, mine))
     send(6, block(0, mine), block(1, mine), twin)
     expect(6, block(1, mine))
+    recv_wait(4)
+    acc = total(e2)
+    norm_all = take(acc, NORM)
+    proj = jnp.where(rid < RHS, acc, 0.0)
+    cor = ((shrink[pl.ds(core * G + g_a, 1), :] - 1.0) * proj).astype(BF).astype(F32)
+    inner = to_row(jnp.sum(cor * proj, axis=1, keepdims=True))
+    corr_own[...] = put(cor, INNER, inner).astype(BF)
+
+    def send3(dev, g):
+        send(5, corr_own, corr.at[:, lanes(core * G + g_a)], dev)
+
+    each(dev_a, send3)
+    expect(5, corr.at[:, pl.ds(0, HALF - L)])
+    corr[:, lanes(core * G + g_a)] = corr_own[...]
+
+    lane = lax.broadcasted_iota(jnp.int32, (L, L), 1)
+
+    def aug_j(lo, hi):
+        def body(n, _):
+            v = sj[lanes(n), 0:L].astype(F32)
+            hi, mid, lo = split3(jnp.broadcast_to(-0.5 * jnp.sum(v * v, axis=1, keepdims=True), (L, L)))
+            ext = jnp.where(lane == 0, hi, jnp.where(lane == 1, mid, jnp.where(lane == 2, lo, 1.0)))
+            sj[lanes(n), L : 2 * L] = jnp.where(lane < 6, ext, 0.0).astype(BF)
+            return 0
+
+        lax.fori_loop(lo, hi, body, 0)
+
+    def aug_i(h, off):
+        W = 512
+        line = lax.broadcasted_iota(jnp.int32, (16, W), 0)
+
+        def body(n, _):
+            d = pl.ds(pl.multiple_of(off + n * W, W), W)
+            v = si[h, 0:L, d].astype(F32)
+            hi, mid, lo = split3(-0.5 * jnp.sum(v * v, axis=0, keepdims=True))
+            ext = jnp.where(line == 3, hi, jnp.where(line == 4, mid, jnp.where(line == 5, lo, 1.0)))
+            si[h, L : L + 16, d] = jnp.where(line < 6, ext, 0.0).astype(BF)
+            return 0
+
+        lax.fori_loop(0, PART // W, body, 0)
+
+    def build(h, off, lo, hi):
+        W = 512
+
+        def body(k, _):
+            e = pl.ds(pl.multiple_of((k // 2) * PART, PART), PART)
+            d = pl.ds(pl.multiple_of(off + (k % 2) * W, W), W)
+            neg = jnp.dot(sj[e, :], si[h, :, d], preferred_element_type=F32)
+            tile[h, e, d] = jnp.exp(jnp.minimum(neg, 0.0)).astype(BF)
+            return 0
+
+        lax.fori_loop(2 * lo, 2 * hi, body, 0)
+
     aug_j(0, 8)
     aug_i(0, mine)
     build(0, mine, 0, 1)
+    recv_wait(6)
+    aug_i(1, mine)
+    build(1, mine, 0, 1)
     recv_wait(5)
     half = corr.at[:, half_of(core)]
     send(7, half, half, twin)
@@ -331,9 +345,6 @@
     recv_wait(14)
     send(15, block(0, rest), block(1, rest), twin)
     expect(15, block(1, rest))
-    recv_wait(6)
-    aug_i(1, mine)
-    build(1, mine, 0, 1)
     recv_wait(13)
     aug_j(8, G)
     build(0, mine, 1, 2)
@@ -418,9 +429,15 @@
         pre, beta, alpha, img = pl.pallas_call(
             kernel,
             out_shape=(out,) * 4,
-            in_specs=[v, v, pl.BlockSpec(memory_space=pl.ANY), v, v, v, v],
+            in_specs=[pl.BlockSpec(memory_space=pl.ANY)] * 7,
             out_specs=(v,) * 4,
             scratch_shapes=[
+                pltpu.VMEM((L, L), BF),
+                pltpu.VMEM((1, L), F32),
+                pltpu.VMEM((rank // L, L), F32),
+                pltpu.VMEM((RHS, L), F32),
+                pltpu.VMEM((RHS, L), F32),
+                pltpu.VMEM((1, RHS), F32),
                 pltpu.VMEM((L, rank), BF),
                 pltpu.VMEM((ROWS, L), F32),
                 pltpu.VMEM((L, L), BF),
@@ -448,6 +465,7 @@
                 pltpu.VMEM((1, L), F32),
                 pltpu.VMEM((2 * G, 1, L), F32),
                 pltpu.SemaphoreType.DMA,
+                pltpu.SemaphoreType.DMA((6,)),
                 pltpu.SemaphoreType.DMA((16,)),
                 pltpu.SemaphoreType.DMA((16,)),
             ],

time: 65.2 us -> 63.4 us (0.972)
  Pallas kernels: 62.7 us -> 61.1 us
    pallas_call x1, Pallas kernels: 62.7 us -> 61.1 us  [step(): pl.pallas_call(kernel, out_shape=(out,) * 4, in_specs=[pl.BlockSpec(memor...]
where the time goes in v5:
time: 63.4 us; the launch traced here: 63.2 us
  Pallas kernels  61.1 us (96%)
  other arithmetic  1.41 us (2%)
  between operations  0.69 us (1%)
    pallas_call x1, Pallas kernels, step(): pl.pallas_call(kernel, out_shape=(out,) * 4, in_specs=[pl.BlockSpec(memor...  61.1 us
    add x1, other arithmetic, step(): return (sol + alpha * direction, res - alpha * img, direction)  1.41 us

profile of v5, /device:TPU:1, one launch (start us, length us, event | category | flops | bytes accessed | tf_op | source)
XLA Modules:
  0.0 63.2 jit_solution(3500865198389450015)
XLA Ops:
  0.6 0.0 copy-start
  0.6 0.0 copy-start.1
  0.7 0.0 copy-start.2
  0.7 61.1 %cg_step.1 = (f32[33,128]{1,0:T(8,128)}, f32[33,128]{1,0:T(8,128)}, f32[33,128]{1,0:T(8,128)}, f32[33,128]{1,0:T(8,128)}) custom-call(bf16[128,128]{1,0:T(8,128)(2,1)} %points_h.1, f32[1,128]{1,0:T(1,128)} %bitcast.4, bf16[128,4096]{1,0:T(8,128)(2,1)} %basis_hbm.1, f32[32,128]{1,0:T(8,128)} %bitcast.3, f32[33,128]{1,0:T(8,128)} %res_h.1, f32[33,128]{1,0:T(8,128)} %prev_h.1, ...), custom_call_target="tpu_custom_call" | custom-call | tf_op jit(solution)/shard_map/cg_step/pallas_call | solution.py:429
  61.7 0.0 copy-done
  61.8 0.0 copy-done.1
  61.8 0.0 copy-done.2
  61.8 1.4 %multiply_add_fusion = (f32[33,128]{1,0:T(8,128)}, f32[33,128]{1,0:T(8,128)}, f32[33,128]{1,0:T(8,128)}) fusion(f32[33,128]{1,0:T(8,128)S(1)} %copy-done.2, f32[33,128]{1,0:T(8,128)} %get-tuple-element.7, f32[33,128]{1,0:T(8,128)} %get-tuple-element.8, f32[33,128]{1,0:T(8,128)} %get-tuple-element.9, f32[33,128]{1,0:T(8,128)S(1)} %copy-done.1, ...), kind=kLoop, calls=%fused_computation.1 | loop fusion | flops 25344 | bytes 168960 | tf_op jit(solution)/shard_map/add | solution.py:481
Async XLA Ops:
  0.6 61.1 %copy-start = (f32[33,128]{1,0:T(8,128)S(1)}, f32[33,128]{1,0:T(8,128)}, u32[]{:S(2)}) copy-start(f32[33,128]{1,0:T(8,128)} %res_h.1) | copy-start | bytes 50692
  0.6 61.1 %copy-start.1 = (f32[33,128]{1,0:T(8,128)S(1)}, f32[33,128]{1,0:T(8,128)}, u32[]{:S(2)}) copy-start(f32[33,128]{1,0:T(8,128)} %prev_h.1) | copy-start | bytes 50692
  0.7 61.1 %copy-start.2 = (f32[33,128]{1,0:T(8,128)S(1)}, f32[33,128]{1,0:T(8,128)}, u32[]{:S(2)}) copy-start(f32[33,128]{1,0:T(8,128)} %param.12) | copy-start | bytes 50692

commit v6 on v5

--- a/solution.py
+++ b/solution.py
@@ -174,9 +174,8 @@
         return pl.ds(pl.multiple_of(c * HALF, HALF), HALF)
 
     proj_t = jnp.dot(r_bf, basis[:, half_of(other)], preferred_element_type=F32)
-    for g in range(G):
-        d = slice(g * L, (g + 1) * L)
-        p_send[:, d] = (proj_t[:, d] + norm_in).astype(BF)
+    p_send[:, 0:L] = (proj_t[:, 0:L] + norm_in).astype(BF)
+    p_send[:, L:HALF] = proj_t[:, L:HALF].astype(BF)
     im_own[...] = jnp.dot(r_bf, basis[:, half_of(core)], preferred_element_type=F32)
 
     pl.semaphore_wait(bar, 2 * (G - 1) + 1)
@@ -237,6 +236,45 @@
     expect(14, block(0, mine))
     send(6, block(0, mine), block(1, mine), twin)
     expect(6, block(1, mine))
+    lane = lax.broadcasted_iota(jnp.int32, (L, L), 1)
+
+    def aug_j(lo, hi):
+        def body(n, _):
+            v = sj[lanes(n), 0:L].astype(F32)
+            hi, mid, lo = split3(jnp.broadcast_to(-0.5 * jnp.sum(v * v, axis=1, keepdims=True), (L, L)))
+            ext = jnp.where(lane == 0, hi, jnp.where(lane == 1, mid, jnp.where(lane == 2, lo, 1.0)))
+            sj[lanes(n), L : 2 * L] = jnp.where(lane < 6, ext, 0.0).astype(BF)
+            return 0
+
+        lax.fori_loop(lo, hi, body, 0)
+
+    def aug_i(h, off):
+        W = 512
+        line = lax.broadcasted_iota(jnp.int32, (16, W), 0)
+
+        def body(n, _):
+            d = pl.ds(pl.multiple_of(off + n * W, W), W)
+            v = si[h, 0:L, d].astype(F32)
+            hi, mid, lo = split3(-0.5 * jnp.sum(v * v, axis=0, keepdims=True))
+            ext = jnp.where(line == 3, hi, jnp.where(line == 4, mid, jnp.where(line == 5, lo, 1.0)))
+            si[h, L : L + 16, d] = jnp.where(line < 6, ext, 0.0).astype(BF)
+            return 0
+
+        lax.fori_loop(0, PART // W, body, 0)
+
+    def build(h, off, lo, hi):
+        d = pl.ds(pl.multiple_of(off, PART), PART)
+
+        def body(k, _):
+            e = pl.ds(pl.multiple_of(k * PART, PART), PART)
+            neg = jnp.dot(sj[e, :], si[h, :, d], preferred_element_type=F32)
+            tile[h, e, d] = jnp.exp(jnp.minimum(neg, 0.0)).astype(BF)
+            return 0
+
+        lax.fori_loop(lo, hi, body, 0)
+
+    aug_j(0, 8)
+    aug_i(0, mine)
     recv_wait(4)
     acc = total(e2)
     norm_all = take(acc, NORM)
@@ -252,46 +290,6 @@
     expect(5, corr.at[:, pl.ds(0, HALF - L)])
     corr[:, lanes(core * G + g_a)] = corr_own[...]
 
-    lane = lax.broadcasted_iota(jnp.int32, (L, L), 1)
-
-    def aug_j(lo, hi):
-        def body(n, _):
-            v = sj[lanes(n), 0:L].astype(F32)
-            hi, mid, lo = split3(jnp.broadcast_to(-0.5 * jnp.sum(v * v, axis=1, keepdims=True), (L, L)))
-            ext = jnp.where(lane == 0, hi, jnp.where(lane == 1, mid, jnp.where(lane == 2, lo, 1.0)))
-            sj[lanes(n), L : 2 * L] = jnp.where(lane < 6, ext, 0.0).astype(BF)
-            return 0
-
-        lax.fori_loop(lo, hi, body, 0)
-
-    def aug_i(h, off):
-        W = 512
-        line = lax.broadcasted_iota(jnp.int32, (16, W), 0)
-
-        def body(n, _):
-            d = pl.ds(pl.multiple_of(off + n * W, W), W)
-            v = si[h, 0:L, d].astype(F32)
-            hi, mid, lo = split3(-0.5 * jnp.sum(v * v, axis=0, keepdims=True))
-            ext = jnp.where(line == 3, hi, jnp.where(line == 4, mid, jnp.where(line == 5, lo, 1.0)))
-            si[h, L : L + 16, d] = jnp.where(line < 6, ext, 0.0).astype(BF)
-            return 0
-
-        lax.fori_loop(0, PART // W, body, 0)
-
-    def build(h, off, lo, hi):
-        W = 512
-
-        def body(k, _):
-            e = pl.ds(pl.multiple_of((k // 2) * PART, PART), PART)
-            d = pl.ds(pl.multiple_of(off + (k % 2) * W, W), W)
-            neg = jnp.dot(sj[e, :], si[h, :, d], preferred_element_type=F32)
-            tile[h, e, d] = jnp.exp(jnp.minimum(neg, 0.0)).astype(BF)
-            return 0
-
-        lax.fori_loop(2 * lo, 2 * hi, body, 0)
-
-    aug_j(0, 8)
-    aug_i(0, mine)
     build(0, mine, 0, 1)
     recv_wait(6)
     aug_i(1, mine)
@@ -312,6 +310,9 @@
     d40[0:RHS, :] = prev[...]
     rz_row = jnp.concatenate([rz[...], jnp.ones((1, L - RHS), F32)], axis=1)
     rz_col = jnp.where(cid < RHS, to_col(rz_row), 1.0)
+    recv_wait(13)
+    aug_j(8, G)
+    build(0, mine, 1, 2)
     recv_wait(7)
     pre = pre + apply(other)
     tail = corr[32:ROWS, 0:L].astype(F32)
@@ -345,9 +346,6 @@
     recv_wait(14)
     send(15, block(0, rest), block(1, rest), twin)
     expect(15, block(1, rest))
-    recv_wait(13)
-    aug_j(8, G)
-    build(0, mine, 1, 2)
     build(1, mine, 1, 2)
     aug_i(0, rest)
     build(0, rest, 0, 2)

time: 63.4 us -> 63.5 us (level)
  no operation moved by 1% of the time
where the time goes in v6:
time: 63.5 us; the launch traced here: 63.2 us
  Pallas kernels  61.1 us (96%)
  other arithmetic  1.41 us (2%)
  between operations  0.69 us (1%)
    pallas_call x1, Pallas kernels, step(): pl.pallas_call(kernel, out_shape=(out,) * 4, in_specs=[pl.BlockSpec(memor...  61.1 us
    add x1, other arithmetic, step(): return (sol + alpha * direction, res - alpha * img, direction)  1.41 us

profile of v6, /device:TPU:1, one launch (start us, length us, event | category | flops | bytes accessed | tf_op | source)
XLA Modules:
  0.0 63.2 jit_solution(9572384760141189103)
XLA Ops:
  0.6 0.0 copy-start
  0.6 0.0 copy-start.1
  0.7 0.0 copy-start.2
  0.7 61.1 %cg_step.1 = (f32[33,128]{1,0:T(8,128)}, f32[33,128]{1,0:T(8,128)}, f32[33,128]{1,0:T(8,128)}, f32[33,128]{1,0:T(8,128)}) custom-call(bf16[128,128]{1,0:T(8,128)(2,1)} %points_h.1, f32[1,128]{1,0:T(1,128)} %bitcast.4, bf16[128,4096]{1,0:T(8,128)(2,1)} %basis_hbm.1, f32[32,128]{1,0:T(8,128)} %bitcast.3, f32[33,128]{1,0:T(8,128)} %res_h.1, f32[33,128]{1,0:T(8,128)} %prev_h.1, ...), custom_call_target="tpu_custom_call" | custom-call | tf_op jit(solution)/shard_map/cg_step/pallas_call | solution.py:427
  61.8 0.0 copy-done
  61.8 0.0 copy-done.1
  61.8 0.0 copy-done.2
  61.8 1.4 %multiply_add_fusion = (f32[33,128]{1,0:T(8,128)}, f32[33,128]{1,0:T(8,128)}, f32[33,128]{1,0:T(8,128)}) fusion(f32[33,128]{1,0:T(8,128)S(1)} %copy-done.2, f32[33,128]{1,0:T(8,128)} %get-tuple-element.7, f32[33,128]{1,0:T(8,128)} %get-tuple-element.8, f32[33,128]{1,0:T(8,128)} %get-tuple-element.9, f32[33,128]{1,0:T(8,128)S(1)} %copy-done.1, ...), kind=kLoop, calls=%fused_computation.1 | loop fusion | flops 25344 | bytes 168960 | tf_op jit(solution)/shard_map/add | solution.py:479
Async XLA Ops:
  0.6 61.1 %copy-start = (f32[33,128]{1,0:T(8,128)S(1)}, f32[33,128]{1,0:T(8,128)}, u32[]{:S(2)}) copy-start(f32[33,128]{1,0:T(8,128)} %res_h.1) | copy-start | bytes 50692
  0.6 61.1 %copy-start.1 = (f32[33,128]{1,0:T(8,128)S(1)}, f32[33,128]{1,0:T(8,128)}, u32[]{:S(2)}) copy-start(f32[33,128]{1,0:T(8,128)} %prev_h.1) | copy-start | bytes 50692
  0.7 61.1 %copy-start.2 = (f32[33,128]{1,0:T(8,128)S(1)}, f32[33,128]{1,0:T(8,128)}, u32[]{:S(2)}) copy-start(f32[33,128]{1,0:T(8,128)} %param.12) | copy-start | bytes 50692
